TPU v7x, 32 devices: a whole 2x2x4 slice. The times are simulated.
32 devices in a mesh: tensor: 4 (over z), frames: 2 (over core), batch: 4 (over y, x).
Axes of the slice: x: 2, y: 2, z: 4, core: 2. Of those that a mesh axis runs over, the one named last changes fastest.
Arguments:
- tokens: bfloat16 [4, 2, 1024, 1024], P('batch', 'frames', 'tensor'), may hold values from -6 to 6
- cotangent: bfloat16 [4, 2, 1024, 1024], P('batch', 'frames', 'tensor'), may hold values from -6 to 6
- bucket: int32 [4], P('batch'), may hold values from 0 to 1, as said below
- clip_of_frame: int32 [4, 8], P('batch'), may hold values from 0 to 6, as said below
- noise_index: int32 [4, 8], P('batch'), may hold values from 0 to 999
- noise_table: float32 [1000, 1024], replicated, may hold values from -6 to 6
- w_mod: bfloat16 [1024, 6144], P(None, 'tensor'), may hold values from -0.1875 to 0.1875
- b_mod: bfloat16 [6144], P('tensor'), may hold values from -1.796875 to 1.796875
- w_qkv: bfloat16 [1024, 3, 1024], P(None, None, 'tensor'), may hold values from -0.1875 to 0.1875
- w_out: bfloat16 [1024, 1024], P('tensor'), may hold values from -1 to 1
- w_up: bfloat16 [1024, 4096], P(None, 'tensor'), may hold values from -0.1875 to 0.1875
- w_down: bfloat16 [4096, 1024], P('tensor'), may hold values from -0.09375 to 0.09375
Outputs:
- out: bfloat16 [4, 2, 1024, 1024], P('batch', 'frames', 'tensor')
- d_tokens: bfloat16 [4, 2, 1024, 1024], P('batch', 'frames', 'tensor')
- d_w_mod: float32 [1024, 6144], P(None, 'tensor')
- d_b_mod: float32 [6144], P('tensor')
- d_w_qkv: float32 [1024, 3, 1024], P(None, None, 'tensor')
- d_w_out: float32 [1024, 1024], P('tensor')
- d_w_up: float32 [1024, 4096], P(None, 'tensor')
- d_w_down: float32 [4096, 1024], P('tensor')
Inputs may be any that keep to these rules, and one draw needn't show every extreme that they name: `bucket`: both values occur in every draw. `clip_of_frame`: A row starts at 0 and never falls; with F the row's frame count (2048 divided by its frame size), frames F // 2 - 1 and F // 2 share a clip; entries from frame F on repeat the clip of frame F - 1. In some pack of 16 by 16 patches every other frame starts a clip of its own. `noise_index`: only a row's first 2048 / (frame size) entries are read.
All inputs are finite; a program needn't handle non-finite values.
Results may differ from a plain program's by a relative error of at most 0.017.
The roundings to bfloat16 on the way count: a program that leaves them out, or rounds other values in their place, can miss the bound.
Values may be sent and summed in bfloat16 or wider, within the bound.
No kernel may reach another device: no remote copies, remote signals or barrier semaphores. Data moves between devices by JAX's collectives and lax.ppermute only.
A program may use at most 192 MiB of HBM per device.

v0:
```python
import jax
import jax.numpy as jnp
from jax import lax
from jax.sharding import PartitionSpec as P

HEAD_DIM = 64
FRAME_SMALL = 256
FRAME_LARGE = 1024


eps = 1e-06
highest = lax.Precision.HIGHEST


def from_behind(value, axis, steps):
    count = lax.axis_size(axis)
    initial, last = (max(0, -steps), min(count, count - steps))
    return lax.ppermute(value, axis, [(source, source + steps) for source in range(initial, last)])


def normalize(values):
    centre = values - jnp.mean(values, axis=-1, keepdims=True)
    spread = jnp.mean(centre * centre, axis=-1, keepdims=True)
    inverse = lax.rsqrt(spread + eps)
    return (centre * inverse, inverse)


def norm_back(grad, normed, inverse):
    mean_grad = jnp.mean(grad, axis=-1, keepdims=True)
    mean_mix = jnp.mean(grad * normed, axis=-1, keepdims=True)
    return inverse * (grad - mean_grad - normed * mean_mix)


def rotary(positions):
    half_dim = HEAD_DIM // 2
    frequency = 10000.0 ** (-(jnp.arange(half_dim, dtype=jnp.float32) * 2.0 / HEAD_DIM))
    angles = positions.astype(jnp.float32)[:, None] * frequency[None, :]
    cosine = jnp.concatenate([jnp.cos(angles), jnp.cos(angles)], axis=-1)[:, None, :]
    sine_table = jnp.concatenate([jnp.sin(angles), jnp.sin(angles)], axis=-1)[:, None, :]
    return (cosine, sine_table)


def rotate(values, cosine, sine_table):
    half_dim = values.shape[-1] // 2
    turned = jnp.concatenate([-values[..., half_dim:], values[..., :half_dim]], axis=-1)
    return values * cosine + turned * sine_table


def gelu_back(pre, grad_hidden):
    return jax.vjp(lambda inner: jax.nn.gelu(inner, approximate=True), pre)[1](grad_hidden)[0]


def spread_rows(rows):
    return lax.all_gather(rows, "tensor", axis=0, tiled=True)


def collect_rows(left_rows, right_matrix, contract):
    return lax.psum_scatter(
        lax.dot_general(
            left_rows,
            right_matrix,
            (((1,), (contract,)), ((), ())),
            preferred_element_type=jnp.float32,
        ),
        "tensor",
        scatter_dimension=0,
        tiled=True,
    )


def masked_scores(query_block, frame_query, clip_query, all_keys, key_frame, key_clip, score_scale):
    allowed = (clip_query[:, None] == key_clip[None, :]) & (
        key_frame[None, :] <= frame_query[:, None]
    )
    scores = (
        jnp.einsum("qhd,khd->hqk", query_block, all_keys, preferred_element_type=jnp.float32)
        * score_scale
    )
    return jnp.where(allowed[None], scores, -1e30)


def attend(
    query_block, frame_query, clip_query, all_keys, all_values, key_frame, key_clip, score_scale
):
    scores = masked_scores(
        query_block, frame_query, clip_query, all_keys, key_frame, key_clip, score_scale
    )
    row_max = jnp.max(scores, axis=-1, keepdims=True)
    weights_exp = jnp.exp(scores - row_max)
    row_total = jnp.sum(weights_exp, axis=-1, keepdims=True)
    probabilities = (weights_exp / row_total).astype(jnp.bfloat16)
    mixed = jnp.einsum(
        "hqk,khd->qhd", probabilities, all_values, preferred_element_type=jnp.float32
    )
    return (mixed, (row_max + jnp.log(row_total))[..., 0])


def attend_back(
    query_block,
    frame_query,
    clip_query,
    grad_mixed,
    log_total,
    all_keys,
    all_values,
    key_frame,
    key_clip,
    score_scale,
):
    scores = masked_scores(
        query_block, frame_query, clip_query, all_keys, key_frame, key_clip, score_scale
    )
    probabilities = jnp.exp(scores - log_total[..., None])
    grad_probs = jnp.einsum(
        "qhd,khd->hqk", grad_mixed, all_values, preferred_element_type=jnp.float32
    )
    centre = jnp.sum(probabilities * grad_probs, axis=-1, keepdims=True)
    grad_scores = (probabilities * (grad_probs - centre)).astype(jnp.bfloat16)
    grad_query = (
        jnp.einsum("hqk,khd->qhd", grad_scores, all_keys, preferred_element_type=jnp.float32)
        * score_scale
    )
    grad_keys = (
        jnp.einsum("hqk,qhd->khd", grad_scores, query_block, preferred_element_type=jnp.float32)
        * score_scale
    )
    grad_values = jnp.einsum(
        "hqk,qhd->khd",
        probabilities.astype(jnp.bfloat16),
        grad_mixed,
        preferred_element_type=jnp.float32,
    )
    return (grad_query, grad_keys, grad_values)


def local(
    tokens,
    cotangent,
    bucket,
    clip_of_frame,
    noise_index,
    noise_table,
    w_mod,
    b_mod,
    w_qkv,
    w_out,
    w_up,
    w_down,
):
    tensor_size = lax.axis_size("tensor")
    tensor_rank = lax.axis_index("tensor")
    frame_rank = lax.axis_index("frames")
    local_rows = tokens.shape[2]
    model_width = tokens.shape[3]
    shard_rows = local_rows * tensor_size
    width_local = w_qkv.shape[2]
    heads_local = width_local // HEAD_DIM
    frame_slots = clip_of_frame.shape[1]
    clip_row = clip_of_frame[0]
    level_row = noise_index[0]
    frame_size = jnp.where(bucket[0] == 0, FRAME_SMALL, FRAME_LARGE).astype(jnp.int32)
    shard_start = frame_rank * shard_rows
    shard_pos = shard_start + jnp.arange(shard_rows, dtype=jnp.int32)
    local_pos = shard_start + tensor_rank * local_rows + jnp.arange(local_rows, dtype=jnp.int32)
    local_frame = local_pos // frame_size
    shard_frame = shard_pos // frame_size
    shard_clip = jnp.take(clip_row, shard_frame)
    past_pos = shard_pos - shard_rows
    past_frame = jnp.maximum(past_pos, 0) // frame_size
    past_clip = jnp.where(past_pos >= 0, jnp.take(clip_row, past_frame), -1)
    key_frame = jnp.concatenate([past_frame, shard_frame])
    key_clip = jnp.concatenate([past_clip, shard_clip])
    cond = jax.nn.silu(jnp.take(noise_table, level_row, axis=0)).astype(jnp.bfloat16)
    mod_part = (
        jnp.dot(cond, w_mod, preferred_element_type=jnp.float32)
        + b_mod.astype(jnp.float32)[None, :]
    )
    mod_whole = lax.all_gather(mod_part, "tensor", axis=1, tiled=True)
    selector = (local_frame[:, None] == jnp.arange(frame_slots, dtype=jnp.int32)[None, :]).astype(
        jnp.float32
    )
    per_token = jnp.dot(selector, mod_whole, precision=highest)
    shift_one = per_token[:, 0:model_width]
    scale_one = per_token[:, model_width : 2 * model_width]
    gate_one = per_token[:, 2 * model_width : 3 * model_width]
    shift_two = per_token[:, 3 * model_width : 4 * model_width]
    scale_two = per_token[:, 4 * model_width : 5 * model_width]
    gate_two = per_token[:, 5 * model_width : 6 * model_width]
    residual = tokens[0, 0].astype(jnp.float32)
    normed_one, inverse_one = normalize(residual)
    attn_in = (normed_one * (1.0 + scale_one) + shift_one).astype(jnp.bfloat16)
    attn_whole = spread_rows(attn_in)
    projected = jnp.einsum("sd,dcf->scf", attn_whole, w_qkv, preferred_element_type=jnp.float32)
    cosine, sine_table = rotary(shard_pos)
    q_raw = projected[:, 0].reshape(shard_rows, heads_local, HEAD_DIM)
    k_raw = projected[:, 1].reshape(shard_rows, heads_local, HEAD_DIM)
    queries = rotate(q_raw, cosine, sine_table).astype(jnp.bfloat16)
    own_keys = rotate(k_raw, cosine, sine_table).astype(jnp.bfloat16)
    own_values = projected[:, 2].reshape(shard_rows, heads_local, HEAD_DIM).astype(jnp.bfloat16)
    past_keys, past_values = from_behind((own_keys, own_values), "frames", 1)
    all_keys = jnp.concatenate([past_keys, own_keys], axis=0)
    all_values = jnp.concatenate([past_values, own_values], axis=0)
    score_scale = HEAD_DIM ** (-0.5)
    block_rows = min(512, shard_rows)
    block_count = shard_rows // block_rows
    query_blocks = queries.reshape(block_count, block_rows, heads_local, HEAD_DIM)
    frame_blocks = shard_frame.reshape(block_count, block_rows)
    clip_blocks = shard_clip.reshape(block_count, block_rows)

    def forward_block(block_items):
        return attend(
            block_items[0],
            block_items[1],
            block_items[2],
            all_keys,
            all_values,
            key_frame,
            key_clip,
            score_scale,
        )

    attn_blocks, total_blocks = lax.map(forward_block, (query_blocks, frame_blocks, clip_blocks))
    attn_rows = attn_blocks.reshape(shard_rows, width_local).astype(jnp.bfloat16)
    branch_one = collect_rows(attn_rows, w_out, 0)
    mixed_one = residual + gate_one * branch_one
    normed_two, inverse_two = normalize(mixed_one)
    mlp_in = (normed_two * (1.0 + scale_two) + shift_two).astype(jnp.bfloat16)
    mlp_whole = spread_rows(mlp_in)
    pre = jnp.dot(mlp_whole, w_up, preferred_element_type=jnp.float32)
    hidden = jax.nn.gelu(pre, approximate=True).astype(jnp.bfloat16)
    branch_two = collect_rows(hidden, w_down, 0)
    result = (mixed_one + gate_two * branch_two).astype(jnp.bfloat16)
    grad_out = cotangent[0, 0].astype(jnp.float32)
    grad_branch_two = (gate_two * grad_out).astype(jnp.bfloat16)
    grad_gate_two = grad_out * branch_two
    grad_two_whole = spread_rows(grad_branch_two)
    mlp_source, _ = lax.optimization_barrier((mlp_in, grad_branch_two))
    mlp_again = spread_rows(mlp_source)
    grad_hidden = lax.dot_general(
        grad_two_whole, w_down, (((1,), (1,)), ((), ())), preferred_element_type=jnp.float32
    )
    grad_pre = gelu_back(pre, grad_hidden).astype(jnp.bfloat16)
    grad_w_down = lax.dot_general(
        hidden, grad_two_whole, (((0,), (0,)), ((), ())), preferred_element_type=jnp.float32
    )
    grad_w_up = lax.dot_general(
        mlp_again, grad_pre, (((0,), (0,)), ((), ())), preferred_element_type=jnp.float32
    )
    grad_mlp_in = collect_rows(grad_pre, w_up, 1)
    grad_scale_two = grad_mlp_in * normed_two
    grad_mixed_one = grad_out + norm_back(grad_mlp_in * (1.0 + scale_two), normed_two, inverse_two)
    grad_branch_one = (gate_one * grad_mixed_one).astype(jnp.bfloat16)
    grad_gate_one = grad_mixed_one * branch_one
    grad_one_whole = spread_rows(grad_branch_one)
    grad_attn = lax.dot_general(
        grad_one_whole, w_out, (((1,), (1,)), ((), ())), preferred_element_type=jnp.float32
    ).astype(jnp.bfloat16)
    grad_w_out = lax.dot_general(
        attn_rows, grad_one_whole, (((0,), (0,)), ((), ())), preferred_element_type=jnp.float32
    )
    grad_attn_blocks = grad_attn.reshape(block_count, block_rows, heads_local, HEAD_DIM)

    def backward_block(carry, block_items):
        query_block, frame_query, clip_query, grad_mixed, log_total = block_items
        grad_query, grad_keys, grad_values = attend_back(
            query_block,
            frame_query,
            clip_query,
            grad_mixed,
            log_total,
            all_keys,
            all_values,
            key_frame,
            key_clip,
            score_scale,
        )
        return ((carry[0] + grad_keys, carry[1] + grad_values), grad_query)

    zero_keys = jnp.zeros((2 * shard_rows, heads_local, HEAD_DIM), jnp.float32)
    key_sums, query_grads = lax.scan(
        backward_block,
        (zero_keys, zero_keys),
        (query_blocks, frame_blocks, clip_blocks, grad_attn_blocks, total_blocks),
    )
    back_keys, back_values = (
        from_behind(key_sums[0][:shard_rows].astype(jnp.bfloat16), "frames", -1).astype(
            jnp.float32
        ),
        from_behind(key_sums[1][:shard_rows].astype(jnp.bfloat16), "frames", -1).astype(
            jnp.float32
        ),
    )
    own_key_grads = key_sums[0][shard_rows:] + back_keys
    own_value_grads = key_sums[1][shard_rows:] + back_values
    grad_q_raw = rotate(query_grads.reshape(shard_rows, heads_local, HEAD_DIM), cosine, -sine_table)
    grad_k_raw = rotate(own_key_grads, cosine, -sine_table)
    grad_qkv = jnp.stack(
        [
            grad_q_raw.reshape(shard_rows, width_local),
            grad_k_raw.reshape(shard_rows, width_local),
            own_value_grads.reshape(shard_rows, width_local),
        ],
        axis=1,
    ).astype(jnp.bfloat16)
    attn_source, _ = lax.optimization_barrier((attn_in, grad_attn))
    attn_again = spread_rows(attn_source)
    grad_w_qkv = jnp.einsum("sd,scf->dcf", attn_again, grad_qkv, preferred_element_type=jnp.float32)
    grad_attn_in = collect_rows(
        grad_qkv.reshape(shard_rows, 3 * width_local),
        w_qkv.reshape(model_width, 3 * width_local),
        1,
    )
    grad_scale_one = grad_attn_in * normed_one
    grad_tokens = grad_mixed_one + norm_back(
        grad_attn_in * (1.0 + scale_one), normed_one, inverse_one
    )
    grad_token_mod = jnp.concatenate(
        [grad_attn_in, grad_scale_one, grad_gate_one, grad_mlp_in, grad_scale_two, grad_gate_two],
        axis=1,
    )
    grad_frame_mod = lax.dot_general(
        selector, grad_token_mod, (((0,), (0,)), ((), ())), precision=highest
    )
    mod_share = lax.psum_scatter(
        grad_frame_mod.astype(jnp.bfloat16), "tensor", scatter_dimension=1, tiled=True
    ).astype(jnp.float32)
    grad_w_mod = lax.dot_general(
        cond.astype(jnp.float32), mod_share, (((0,), (0,)), ((), ())), precision=highest
    )
    grad_b_mod = jnp.sum(mod_share, axis=0)
    summed = (
        lax.psum(grad_w_mod.astype(jnp.bfloat16), ("frames", "batch")).astype(jnp.float32),
        lax.psum(grad_b_mod.astype(jnp.bfloat16), ("frames", "batch")).astype(jnp.float32),
        lax.psum(grad_w_qkv.astype(jnp.bfloat16), ("frames", "batch")).astype(jnp.float32),
        lax.psum(grad_w_out.astype(jnp.bfloat16), ("frames", "batch")).astype(jnp.float32),
        lax.psum(grad_w_up.astype(jnp.bfloat16), ("frames", "batch")).astype(jnp.float32),
        lax.psum(grad_w_down.astype(jnp.bfloat16), ("frames", "batch")).astype(jnp.float32),
    )
    return (
        result.reshape(1, 1, local_rows, model_width),
        grad_tokens.astype(jnp.bfloat16).reshape(1, 1, local_rows, model_width),
        summed[0],
        summed[1],
        summed[2],
        summed[3],
        summed[4],
        summed[5],
    )


def solution(mesh):
    placed = (
        P("batch", "frames", "tensor", None),
        P("batch", "frames", "tensor", None),
        P("batch"),
        P("batch", None),
        P("batch", None),
        P(),
        P(None, "tensor"),
        P("tensor"),
        P(None, None, "tensor"),
        P("tensor", None),
        P(None, "tensor"),
        P("tensor", None),
    )
    return jax.shard_map(
        local,
        mesh=mesh,
        in_specs=placed,
        out_specs=(
            P("batch", "frames", "tensor", None),
            P("batch", "frames", "tensor", None),
            P(None, "tensor"),
            P("tensor"),
            P(None, None, "tensor"),
            P("tensor", None),
            P(None, "tensor"),
            P("tensor", None),
        ),
        check_vma=False,
    )
```

profile of v0, /device:TPU:0, one launch (start us, length us, event | category | flops | bytes accessed | tf_op | source)
XLA Modules:
  0.0 981.8 jit_solution(5190104987393337398)
XLA Ops:
  16.0 15.6 %all_gather.21 = f32[8,6144]{1,0:T(8,128)S(1)} all-gather(f32[8,1536]{1,0:T(8,128)S(1)} %convolution_add_fusion), channel_id=1, replica_groups=mesh['tensor'=4,'frames'=2,'batch'=4] {'tensor'}, dimensions={1}, use_global_device_ids=true | all-gather | bytes 245760 | tf_op jit(solution)/shard_map/all_gather | solution.py:178
  39.1 5.3 select_select_fusion
  51.4 34.1 %all-gather.7.cloned.1.call-done = bf16[1024,1024]{1,0:T(8,128)(2,1)} async-done(((bf16[256,1024]{1,0:T(8,128)(2,1)}), bf16[1024,1024]{1,0:T(8,128)(2,1)}) %all-gather.7.cloned.1.call-update) | async-done | bytes 2097168 | tf_op jit(solution)/shard_map/all_gather | solution.py:54
  85.5 3.5 fusion.50
  104.5 29.2 %while.29 = (s32[]{:T(128)}, bf16[2,512,4,64]{1,3,2,0:T(8,128)(2,1)S(1)}, f32[2,4,512]{2,1,0:T(4,128)}, s32[2,512]{1,0:T(2,128)S(1)}, s32[2048]{0:T(1024)S(1)}, ...) while((s32[]{:T(128)}, ...), condition=%wide.region_5.7_spmd.clone, body=%wide.region_2.6_spmd.sunk.clone | while | flops 1127217152 | bytes 57503868 | solution.py:222
  106.1 3.3 fusion.176
  109.4 4.3 fusion.177
  113.7 4.8 fusion.178
  120.7 3.3 fusion.176
  124.0 4.3 fusion.177
  128.3 4.8 fusion.178
  135.1 3.8 fusion.106
  139.0 75.9 %reduce-scatter.6.cloned.1.call-done = f32[256,1024]{1,0:T(8,128)} async-done(((f32[1024,1024]{1,0:T(8,128)}), f32[256,1024]{1,0:T(8,128)}) %reduce-scatter.6.cloned.1.call-update) | async-done | bytes 1048592 | tf_op jit(solution)/shard_map/reduce_scatter | solution.py:58
  217.7 3.1 fusion.72
  221.9 45.3 %all-gather.11.cloned.1.call-done = bf16[1024,1024]{1,0:T(8,128)(2,1)} async-done(((bf16[256,1024]{1,0:T(8,128)(2,1)}), bf16[1024,1024]{1,0:T(8,128)(2,1)}) %all-gather.11.cloned.1.call-update) | async-done | bytes 2097168 | tf_op jit(solution)/shard_map/all_gather | solution.py:54
  267.2 6.6 fusion.107
  273.8 39.3 %all-gather.9.cloned.1.call-done = bf16[1024,1024]{1,0:T(8,128)(2,1)} async-done(((bf16[256,1024]{1,0:T(8,128)(2,1)}), bf16[1024,1024]{1,0:T(8,128)(2,1)}) %all-gather.9.cloned.1.call-update) | async-done | bytes 2097168 | tf_op jit(solution)/shard_map/all_gather | solution.py:54
  313.1 10.0 %fusion.47 = (bf16[1024,1024]{1,0:T(8,128)(2,1)S(1)}, f32[1024,1024]{1,0:T(8,128)}) fusion(f32[1024,1024]{1,0:T(8,128)} %fusion.107, bf16[1024,1024]{1,0:T(8,128)(2,1)} %all-gather.9.cloned.1.call-done, bf16[1024,1024]{1,0:T(8,128)(2,1)} %param.28), kind=kOutput, calls=%fused_computation.62 | convolution fusion | flops 2168455168 | bytes 14680064 | tf_op jit(solution)/shard_map/dot_general | solution.py:229
  324.4 4.4 fusion.108
  328.9 7.5 fusion.101
  336.5 68.1 %reduce-scatter.10.cloned.1.call-done = f32[256,1024]{1,0:T(8,128)} async-done(((f32[1024,1024]{1,0:T(8,128)}), f32[256,1024]{1,0:T(8,128)}) %reduce-scatter.10.cloned.1.call-update) | async-done | bytes 1048592 | tf_op jit(solution)/shard_map/reduce_scatter | solution.py:58
  406.8 77.3 %reduce-scatter.8.cloned.1.call-done = f32[256,1024]{1,0:T(8,128)} async-done(((f32[1024,1024]{1,0:T(8,128)}), f32[256,1024]{1,0:T(8,128)}) %reduce-scatter.8.cloned.1.call-update) | async-done | bytes 1048592 | tf_op jit(solution)/shard_map/reduce_scatter | solution.py:58
  484.1 4.7 multiply_convert_fusion.2
  489.6 45.5 %all-gather.13.cloned.1.call-done = bf16[1024,1024]{1,0:T(8,128)(2,1)} async-done(((bf16[256,1024]{1,0:T(8,128)(2,1)}), bf16[1024,1024]{1,0:T(8,128)(2,1)}) %all-gather.13.cloned.1.call-update) | async-done | bytes 2097168 | tf_op jit(solution)/shard_map/all_gather | solution.py:54
  541.2 94.7 %while.30 = (s32[]{:T(128)}, f32[2048,4,64]{0,2,1:T(8,128)}, f32[2048,4,64]{0,2,1:T(8,128)}, f32[2,512,4,64]{1,3,2,0:T(8,128)}, bf16[2,512,4,64]{1,3,2,0:T(8,128...) while((s32[]{:T(128)}, f32[2048,4,64]{0,2,1:T(8,128)}, ...), condition=%wide.region_15.17_spmd.clone.clone, body=%wide.region_13.16_spmd.clone.sunk.clone | while | flops 2753165312 | bytes 195776976 | solution.py:280
  544.5 3.6 fusion.188
  548.1 6.3 fusion.190
  554.4 11.6 %multiply_reduce_fusion.5 = (f32[4,512]{1,0:T(4,128)}, f32[4,512,2048]{2,1,0:T(8,128)}) fusion(f32[4,512,2048]{2,1,0:T(8,128)S(1)} %fusion.188, f32[4,512]{1,0:T(4,128)S(1)} %dynamic-slice_bitcast_fusion.3, pred[512,2048]{1,0:T(8,128)(4,1)} %copy-done.3, bf16[2048,4,64]{0,2,1:T(8,128)(2,1)} %copy-done.8, ...), kind=kOutput, calls=%fused_computation.20.clone.1.clone | convolution fusion | flops 557840384 | bytes 35930116 | tf_op jit(solution)/shard_map/while/body/eval_jaxpr/qhd,khd->hqk/dot_general | solution.py:114
  566.0 11.0 %multiply_convert_fusion.10 = bf16[4,512,2048]{2,1,0:T(8,128)(2,1)} fusion(f32[4,512,2048]{2,1,0:T(8,128)} %get-tuple-element.524, f32[4,512,2048]{2,1,0:T(8,128)S(1)} %fusion.188, f32[4,512]{1,0:T(4,128)} %get-tuple-element.525, f32[4,512]{1,0:T(4,128)S(1)} %dynamic-slice_bitcast_fusion.3, pred[512,2048]{1,0:T(8,128)(4,1)} %copy-done.3), kind=kLoop, calls=%fused_computation.19.clone.1.clone | loop fusion | flops 25165824 | bytes 43008000 | tf_op jit(solution)/shard_map/while/body/eval_jaxpr/convert_element_type | solution.py:118
  577.1 7.1 fusion.191
  590.2 3.6 fusion.188
  593.9 7.5 fusion.190
  601.4 11.6 %multiply_reduce_fusion.5 = (f32[4,512]{1,0:T(4,128)}, f32[4,512,2048]{2,1,0:T(8,128)}) fusion(f32[4,512,2048]{2,1,0:T(8,128)S(1)} %fusion.188, f32[4,512]{1,0:T(4,128)S(1)} %dynamic-slice_bitcast_fusion.3, pred[512,2048]{1,0:T(8,128)(4,1)} %copy-done.3, bf16[2048,4,64]{0,2,1:T(8,128)(2,1)} %copy-done.8, ...), kind=kOutput, calls=%fused_computation.20.clone.1.clone | convolution fusion | flops 557840384 | bytes 35930116 | tf_op jit(solution)/shard_map/while/body/eval_jaxpr/qhd,khd->hqk/dot_general | solution.py:114
  613.0 11.0 %multiply_convert_fusion.10 = bf16[4,512,2048]{2,1,0:T(8,128)(2,1)} fusion(f32[4,512,2048]{2,1,0:T(8,128)} %get-tuple-element.524, f32[4,512,2048]{2,1,0:T(8,128)S(1)} %fusion.188, f32[4,512]{1,0:T(4,128)} %get-tuple-element.525, f32[4,512]{1,0:T(4,128)S(1)} %dynamic-slice_bitcast_fusion.3, pred[512,2048]{1,0:T(8,128)(4,1)} %copy-done.3), kind=kLoop, calls=%fused_computation.19.clone.1.clone | loop fusion | flops 25165824 | bytes 43008000 | tf_op jit(solution)/shard_map/while/body/eval_jaxpr/convert_element_type | solution.py:118
  624.0 7.0 fusion.191
  631.0 4.6 fusion.189
  665.7 5.6 convolution_bitcast_fusion
  672.9 6.4 convolution_convert_fusion.2
  679.6 5.9 convolution_convert_fusion.3
  685.6 3.2 convolution_convert_fusion.4
  688.8 60.6 %reduce-scatter.12.cloned.1.call-done = f32[256,1024]{1,0:T(8,128)} async-done(((f32[1024,1024]{1,0:T(8,128)}), f32[256,1024]{1,0:T(8,128)}) %reduce-scatter.12.cloned.1.call-update) | async-done | bytes 1048592 | tf_op jit(solution)/shard_map/reduce_scatter | solution.py:58
  758.7 38.2 %all-gather.15.cloned.1.call-done = bf16[1024,1024]{1,0:T(8,128)(2,1)} async-done(((bf16[256,1024]{1,0:T(8,128)(2,1)}), bf16[1024,1024]{1,0:T(8,128)(2,1)}) %all-gather.15.cloned.1.call-update) | async-done | bytes 2097168 | tf_op jit(solution)/shard_map/all_gather | solution.py:54
  797.0 4.6 fusion.52
  801.6 16.4 %reduce-scatter.14.cloned.1.call-done = bf16[8,1536]{1,0:T(8,128)(2,1)} async-done(((bf16[8,6144]{1,0:T(8,128)(2,1)}), bf16[8,1536]{1,0:T(8,128)(2,1)}) %reduce-scatter.14.cloned.1.call-update) | async-done | bytes 24592 | tf_op jit(solution)/shard_map/reduce_scatter | solution.py:324
  818.0 3.5 convolution_convert_fusion.1
  822.3 15.2 %psum.43 = bf16[1536]{0:T(1024)(128)(2,1)S(1)} all-reduce(bf16[1536]{0:T(1024)(128)(2,1)S(1)} %reduce_sum.110), channel_id=1, replica_groups=mesh['tensor'=4,'frames'=2,'batch'=4] {'frames','batch'}, use_global_device_ids=true, to_apply=%region_22.24 | all-reduce | flops 1536 | bytes 6144 | tf_op jit(solution)/shard_map/psum | solution.py:333
  838.1 121.2 %all-reduce.3.cloned.1.call-done = (bf16[1024,1536]{1,0:T(8,128)(2,1)}, bf16[1024,3,256]{2,0,1:T(8,128)(2,1)}, bf16[256,1024]{1,0:T(8,128)(2,1)}, bf16[1024,1024]{1,0:T(8,128)(2,1)}, bf16[1024,1024]{1,0:T(8,128)(2,1)}) async-done(((bf16[1024,1536]{1,0:T(8,128)(2,1)}, bf16[1024,3,256]{2,0,1:T(8,128)(2,1)}, bf16[256,1024]{1,0:T(8,128)(2,1)}, bf16[1024,1024]{1,0:T(8,128)(2,1)}, bf16[1024,1024]{1,0:T(8,128)(2,1)}), ...) | async-done | bytes 9437200 | tf_op jit(solution)/shard_map/psum | solution.py:332
  961.4 5.6 convert_element_type.156
  (290 shorter events, 118.9 us)
Async XLA Ops:
  7.2 8.3 copy-start
  7.2 78.3 %all-gather.7.cloned.1.call-start = ((), (), s32[]{:S(2)}) async-start(), calls=%async_computation.5 | async-start | bytes 2621440 | tf_op jit(solution)/shard_map/all_gather | solution.py:54
  8.0 26.4 %copy-start.62 = (pred[8]{0:T(512)(128)(4,1)}, pred[8]{0:T(512)(128)(4,1)S(1)}, u32[]{:S(2)}) copy-start(pred[8]{0:T(512)(128)(4,1)S(1)} %compare_and_fusion.2) | copy-start | bytes 28
  10.6 23.8 %copy-start.54 = (f32[256]{0:T(256)}, f32[256]{0:T(256)S(1)}, u32[]{:S(2)}) copy-start(f32[256]{0:T(256)S(1)} %broadcast_multiply_fusion.5) | copy-start | bytes 3076
  12.0 22.5 %copy-start.58 = (f32[256]{0:T(256)}, f32[256]{0:T(256)S(1)}, u32[]{:S(2)}) copy-start(f32[256]{0:T(256)S(1)} %add_rsqrt_fusion.1) | copy-start | bytes 3076
  15.5 19.0 %copy-start.48 = (f32[8,1024]{1,0:T(8,128)}, f32[8,1024]{1,0:T(8,128)S(1)}, u32[]{:S(2)}) copy-start(f32[8,1024]{1,0:T(8,128)S(1)} %gather_fusion) | copy-start | bytes 98308
  16.0 21.2 %copy-start.12 = (bf16[1,1,256,1024]{3,2,1,0:T(8,128)(2,1)S(1)}, bf16[1,1,256,1024]{3,2,1,0:T(8,128)(2,1)}, u32[]{:S(2)}) copy-start(bf16[1,1,256,1024]{3,2,1,0:T(8,128)(2,1)} %param.18) | copy-start | bytes 1572868
  31.8 6.6 copy-start.60
  31.8 6.6 copy-start.53
  37.2 48.3 %copy-start.66 = (bf16[1024,3,256]{2,0,1:T(8,128)(2,1)S(1)}, bf16[1024,3,256]{2,0,1:T(8,128)(2,1)}, u32[]{:S(2)}) copy-start(bf16[1024,3,256]{2,0,1:T(8,128)(2,1)} %param.26) | copy-start | bytes 4718596
  38.4 176.6 %reduce-scatter.6.cloned.1.call-start = ((), (), s32[]{:S(2)}) async-start(), calls=%async_computation.6 | async-start | bytes 5242880 | tf_op jit(solution)/shard_map/reduce_scatter | solution.py:58
  51.4 46.9 %copy-start.23 = (f32[1024,64]{0,1:T(8,128)}, f32[1024,64]{0,1:T(8,128)S(1)}, u32[]{:S(2)}) copy-start(f32[1024,64]{0,1:T(8,128)S(1)} %get-tuple-element.325) | copy-start | bytes 786436
  90.1 13.0 %collective-permute-start.1 = (bf16[1024,4,64]{0,2,1:T(8,128)(2,1)}, bf16[1024,4,64]{0,2,1:T(8,128)(2,1)}, u32[]{:S(2)}, u32[]{:S(2)}) collective-permute-start(bf16[1024,4,64]{0,2,1:T(8,128)(2,1)} %bitcast.31), channel_id=1, source_target_pairs={{0,4},{1,5},{2,6},{3,7},{8,12},{9,13},{10,14},{11,15},{16,20},{17,... | collective-permute-start | bytes 1572872 | tf_op jit(solution)/shard_map/ppermute | solution.py:18
  99.5 4.8 collective-permute-start
  138.9 76.0 %copy-start.13 = (bf16[1,1,256,1024]{3,2,1,0:T(8,128)(2,1)S(1)}, bf16[1,1,256,1024]{3,2,1,0:T(8,128)(2,1)}, u32[]{:S(2)}) copy-start(bf16[1,1,256,1024]{3,2,1,0:T(8,128)(2,1)} %param.18) | copy-start | bytes 1572868
  138.9 128.2 %all-gather.11.cloned.1.call-start = ((), (), s32[]{:S(2)}) async-start(), calls=%async_computation.9 | async-start | bytes 2621440 | tf_op jit(solution)/shard_map/all_gather | solution.py:54
  216.7 267.3 %copy-start.51 = (f32[256]{0:T(256)}, f32[256]{0:T(256)S(1)}, u32[]{:S(2)}) copy-start(f32[256]{0:T(256)S(1)} %broadcast_multiply_fusion.4) | copy-start | bytes 3076
  217.7 266.4 %copy-start.56 = (f32[256]{0:T(256)}, f32[256]{0:T(256)S(1)}, u32[]{:S(2)}) copy-start(f32[256]{0:T(256)S(1)} %add_rsqrt_fusion) | copy-start | bytes 3076
  220.8 92.2 %all-gather.9.cloned.1.call-start = ((), (), s32[]{:S(2)}) async-start(), calls=%async_computation.7 | async-start | bytes 2621440 | tf_op jit(solution)/shard_map/all_gather | solution.py:54
  221.4 183.2 %reduce-scatter.10.cloned.1.call-start = ((), (), s32[]{:S(2)}) async-start(), calls=%async_computation.10 | async-start | bytes 5242880 | tf_op jit(solution)/shard_map/reduce_scatter | solution.py:58
  313.1 11.4 %copy-start.64 = (bf16[1024,1024]{1,0:T(8,128)(2,1)S(1)}, bf16[1024,1024]{1,0:T(8,128)(2,1)}, u32[]{:S(2)}) copy-start(bf16[1024,1024]{1,0:T(8,128)(2,1)} %param.28) | copy-start | bytes 6291460
  328.8 155.2 %reduce-scatter.8.cloned.1.call-start = ((), (), s32[]{:S(2)}) async-start(), calls=%async_computation.8 | async-start | bytes 5242880 | tf_op jit(solution)/shard_map/reduce_scatter | solution.py:58
  336.4 147.7 %copy-start.19 = (bf16[1,1,256,1024]{3,2,1,0:T(8,128)(2,1)S(1)}, bf16[1,1,256,1024]{3,2,1,0:T(8,128)(2,1)}, u32[]{:S(2)}) copy-start(bf16[1,1,256,1024]{3,2,1,0:T(8,128)(2,1)} %param.19) | copy-start | bytes 1572868
  336.4 198.7 %all-gather.13.cloned.1.call-start = ((), (), s32[]{:S(2)}) async-start(), calls=%async_computation.11 | async-start | bytes 2621440 | tf_op jit(solution)/shard_map/all_gather | solution.py:54
  488.8 190.8 %all-gather.17.cloned.1.call-start = ((), (), s32[]{:S(2)}) async-start(), calls=%async_computation.15 | async-start | bytes 2621440 | tf_op jit(solution)/shard_map/all_gather | solution.py:54
  489.6 259.8 %reduce-scatter.12.cloned.1.call-start = ((), (), s32[]{:S(2)}) async-start(), calls=%async_computation.12 | async-start | bytes 5242880 | tf_op jit(solution)/shard_map/reduce_scatter | solution.py:58
  577.1 7.1 copy-start.2
  577.1 7.1 copy-start.7
  624.0 7.0 copy-start.2
  624.0 7.0 copy-start.7
  635.9 8.1 copy-start.4
  635.9 10.3 %copy-start.22 = (f32[2,512,4,64]{1,3,2,0:T(8,128)S(1)}, f32[2,512,4,64]{1,3,2,0:T(8,128)}, u32[]{:S(2)}) copy-start(f32[2,512,4,64]{1,3,2,0:T(8,128)} %get-tuple-element.135) | copy-start | bytes 3145732
  638.2 15.6 %collective-permute-start.3 = (bf16[1024,4,64]{0,2,1:T(8,128)(2,1)}, bf16[1024,4,64]{0,2,1:T(8,128)(2,1)}, u32[]{:S(2)}, u32[]{:S(2)}) collective-permute-start(bf16[1024,4,64]{0,2,1:T(8,128)(2,1)} %slice.183), channel_id=1, source_target_pairs={{4,0},{5,1},{6,2},{7,3},{12,8},{13,9},{14,10},{15,11},{20,16},{21,... | collective-permute-start | bytes 1572872 | tf_op jit(solution)/shard_map/ppermute | solution.py:18
  644.9 13.3 %collective-permute-start.2 = (bf16[1024,4,64]{0,2,1:T(8,128)(2,1)}, bf16[1024,4,64]{0,2,1:T(8,128)(2,1)}, u32[]{:S(2)}, u32[]{:S(2)}) collective-permute-start(bf16[1024,4,64]{0,2,1:T(8,128)(2,1)} %slice.184), channel_id=1, source_target_pairs={{4,0},{5,1},{6,2},{7,3},{12,8},{13,9},{14,10},{15,11},{20,16},{21,... | collective-permute-start | bytes 1572872 | tf_op jit(solution)/shard_map/ppermute | solution.py:18
  671.3 125.7 %all-gather.15.cloned.1.call-start = ((), (), s32[]{:S(2)}) async-start(), calls=%async_computation.14 | async-start | bytes 2621440 | tf_op jit(solution)/shard_map/all_gather | solution.py:54
  679.3 6.3 copy-start.29
  679.3 70.1 %copy-start.14 = (bf16[1,1,256,1024]{3,2,1,0:T(8,128)(2,1)S(1)}, bf16[1,1,256,1024]{3,2,1,0:T(8,128)(2,1)}, u32[]{:S(2)}) copy-start(bf16[1,1,256,1024]{3,2,1,0:T(8,128)(2,1)} %param.18) | copy-start | bytes 1572868
  679.3 70.1 %copy-start.55 = (f32[256]{0:T(256)S(1)}, f32[256]{0:T(256)}, u32[]{:S(2)}) copy-start(f32[256]{0:T(256)} %copy-done.54) | copy-start | bytes 3076
  679.3 70.1 %copy-start.59 = (f32[256]{0:T(256)S(1)}, f32[256]{0:T(256)}, u32[]{:S(2)}) copy-start(f32[256]{0:T(256)} %copy-done.58) | copy-start | bytes 3076
  679.3 138.7 %reduce-scatter.14.cloned.1.call-start = ((), (), s32[]{:S(2)}) async-start(), calls=%async_computation.13 | async-start | bytes 122880 | tf_op jit(solution)/shard_map/reduce_scatter | solution.py:324
  685.6 65.9 %copy-start.16 = (f32[256,1024]{1,0:T(8,128)S(1)}, f32[256,1024]{1,0:T(8,128)}, u32[]{:S(2)}) copy-start(f32[256,1024]{1,0:T(8,128)} %get-tuple-element.274) | copy-start | bytes 3145732
  688.8 65.4 %copy-start.25 = (f32[256,1024]{1,0:T(8,128)S(1)}, f32[256,1024]{1,0:T(8,128)}, u32[]{:S(2)}) copy-start(f32[256,1024]{1,0:T(8,128)} %reduce-scatter.6.cloned.1.call-done) | copy-start | bytes 3145732
  755.5 41.4 %copy-start.44 = (bf16[1024,1,256]{2,0,1:T(8,128)(2,1)S(1)}, bf16[1024,1,256]{2,0,1:T(8,128)(2,1)}, u32[]{:S(2)}) copy-start(bf16[1024,1,256]{2,0,1:T(8,128)(2,1)} %copy-done.43) | copy-start | bytes 1572868
  755.5 41.4 %copy-start.46 = (bf16[1024,1,256]{2,0,1:T(8,128)(2,1)S(1)}, bf16[1024,1,256]{2,0,1:T(8,128)(2,1)}, u32[]{:S(2)}) copy-start(bf16[1024,1,256]{2,0,1:T(8,128)(2,1)} %copy.41) | copy-start | bytes 1572868
  755.5 41.4 %copy-start.47 = (bf16[1024,1,256]{2,0,1:T(8,128)(2,1)S(1)}, bf16[1024,1,256]{2,0,1:T(8,128)(2,1)}, u32[]{:S(2)}) copy-start(bf16[1024,1,256]{2,0,1:T(8,128)(2,1)} %copy.40) | copy-start | bytes 1572868
  758.7 59.4 %copy-start.49 = (f32[8,1024]{1,0:T(8,128)S(1)}, f32[8,1024]{1,0:T(8,128)}, u32[]{:S(2)}) copy-start(f32[8,1024]{1,0:T(8,128)} %copy-done.48) | copy-start | bytes 98308
  758.7 59.3 %copy-start.63 = (pred[8]{0:T(512)(128)(4,1)S(1)}, pred[8]{0:T(512)(128)(4,1)}, u32[]{:S(2)}) copy-start(pred[8]{0:T(512)(128)(4,1)} %copy-done.62) | copy-start | bytes 28
  758.7 200.6 %all-reduce.3.cloned.1.call-start = ((), (), s32[]{:S(2)}) async-start(), calls=%async_computation.16 | async-start | bytes 18874368 | tf_op jit(solution)/shard_map/psum | solution.py:332
  (47 other events, 123.9 us)
Sparse Core Ops, SparseCore 0:
  38.5 46.9 all-gather.6
  139.1 75.8 reduce-scatter.5
  221.0 46.1 all-gather.10
  268.6 44.4 all-gather.8
  329.0 75.5 reduce-scatter.9
  406.7 77.2 reduce-scatter.7
  488.9 46.1 all-gather.12
  536.7 44.4 all-gather.16
  671.4 77.9 reduce-scatter.11
  750.8 46.1 all-gather.14
  799.8 18.1 reduce-scatter.13
  822.9 136.2 all-reduce.2
where the time goes:
time: 991 us; the launch traced here: 982 us
  waiting for transfers between devices  623 us (63%)
  matrix products  156 us (16%)
  other arithmetic  102 us (10%)
  local copies, waits for them, and re-layouts  45.5 us (5%)
  blocking collectives  30.8 us (3%)
  between operations  16.1 us (2%)
    reduce_scatter x4, waiting for transfers between devices, collect_rows(): lax.psum_scatter(lax.dot_general(left_rows, right_matrix, (((1,), (contra...  282 us
    all_gather x6, waiting for transfers between devices, spread_rows(): return lax.all_gather(rows, 'tensor', axis=0, tiled=True)  202 us
    psum x1, waiting for transfers between devices, local(): lax.psum(grad_w_mod.astype(jnp.bfloat16), ('frames', 'batch'))  121 us
    dot_general x2, matrix products, attend_back(): jnp.einsum('qhd,khd->hqk', grad_mixed, all_values, preferred_element_type...  23.3 us
    convert_element_type x2, other arithmetic, attend_back(): grad_scores = (probabilities * (grad_probs - centre)).astype(jnp.bfloat16)  22 us
    dot_general x4, matrix products, collect_rows(): lax.dot_general(left_rows, right_matrix, (((1,), (contract,)), ((), ())),...  21.3 us
  transfers between devices with their start and end apart: 16, of which 11 were waited for; matrix products, arithmetic and copies ran while one was open for 20% of the time, Pallas kernels for 0%

commit v1 on v0

v1 whole, which is shorter than its diff:
```python
import functools

import jax
import jax.numpy as jnp
from jax import lax
from jax.experimental import pallas as pl
from jax.experimental.pallas import tpu as pltpu
from jax.sharding import PartitionSpec as P

HEAD_DIM = 64
FRAME_SMALL = 256
FRAME_LARGE = 1024
BLOCK = 256
LOG2E = 1.4426950408889634
SCALE = HEAD_DIM ** (-0.5)

eps = 1e-06
highest = lax.Precision.HIGHEST
f32 = jnp.float32
bf16 = jnp.bfloat16


def normalize(values):
    centre = values - jnp.mean(values, axis=-1, keepdims=True)
    spread = jnp.mean(centre * centre, axis=-1, keepdims=True)
    inverse = lax.rsqrt(spread + eps)
    return (centre * inverse, inverse)


def norm_back(grad, normed, inverse):
    mean_grad = jnp.mean(grad, axis=-1, keepdims=True)
    mean_mix = jnp.mean(grad * normed, axis=-1, keepdims=True)
    return inverse * (grad - mean_grad - normed * mean_mix)


def rotary_tables(positions, width):
    half_dim = HEAD_DIM // 2
    frequency = 10000.0 ** (-(jnp.arange(half_dim, dtype=f32) * 2.0 / HEAD_DIM))
    angles = positions.astype(f32)[:, None] * frequency[None, :]
    cosine = jnp.cos(angles)
    sine = jnp.sin(angles)
    copies = width // HEAD_DIM
    return (
        jnp.concatenate([cosine, cosine] * copies, axis=-1),
        jnp.concatenate([-sine, sine] * copies, axis=-1),
    )


def turn(values):
    half = HEAD_DIM // 2
    width = values.shape[-1]
    if width % 128 == 0:
        lane = lax.broadcasted_iota(jnp.int32, values.shape, 1)
        first = (lane % HEAD_DIM) < half
        return jnp.where(
            first, pltpu.roll(values, width - half, 1), pltpu.roll(values, half, 1)
        )
    pieces = []
    for at in range(0, width, HEAD_DIM):
        pieces += [values[:, at + half : at + HEAD_DIM], values[:, at : at + half]]
    return jnp.concatenate(pieces, axis=-1)


def project_kernel(frame_ref, x_ref, mod_ref, w_ref, cos_ref, sin_ref, in_ref, out_ref):
    block = pl.program_id(0)
    width = x_ref.shape[1]
    group = cos_ref.shape[1]
    row = mod_ref[pl.ds(frame_ref[block], 1), :]
    normed, _ = normalize(x_ref[...].astype(f32))
    attn_in = (normed * (1.0 + row[:, width : 2 * width]) + row[:, :width]).astype(bf16)
    in_ref[...] = attn_in
    projected = jnp.dot(attn_in, w_ref[...], preferred_element_type=f32)
    cosine, sine = cos_ref[...], sin_ref[...]
    for side in range(2):
        for kind in range(3):
            at = (side * 3 + kind) * group
            part = projected[:, at : at + group]
            if kind < 2:
                part = part * cosine + turn(part) * sine
            out_ref[side, kind] = part.astype(bf16)


def project(frames, tokens, mod, weights, cosine, sine):
    rows, width = tokens.shape
    columns = weights.shape[1]
    group = cosine.shape[1]
    whole = lambda i, fr: (0, 0)
    return pl.pallas_call(
        project_kernel,
        grid_spec=pltpu.PrefetchScalarGridSpec(
            num_scalar_prefetch=1,
            grid=(rows // BLOCK,),
            in_specs=[
                pl.BlockSpec((BLOCK, width), lambda i, fr: (i, 0)),
                pl.BlockSpec(mod.shape, whole),
                pl.BlockSpec((width, columns), whole),
                pl.BlockSpec((BLOCK, group), lambda i, fr: (i, 0)),
                pl.BlockSpec((BLOCK, group), lambda i, fr: (i, 0)),
            ],
            out_specs=[
                pl.BlockSpec((BLOCK, width), lambda i, fr: (i, 0)),
                pl.BlockSpec((2, 3, BLOCK, group), lambda i, fr: (0, 0, i, 0)),
            ],
        ),
        out_shape=[
            jax.ShapeDtypeStruct((rows, width), bf16),
            jax.ShapeDtypeStruct((2, 3, rows, group), bf16),
        ],
        name="project",
    )(frames, tokens, mod, weights, cosine, sine)


def only_head(values, head, axis):
    place = lax.broadcasted_iota(jnp.int32, values.shape, axis) // HEAD_DIM
    return jnp.where(place == head, values, jnp.zeros_like(values))


def key_loop(lo_ref, hi_ref, flag_ref, block, body, carry):
    lo, hi = lo_ref[block], hi_ref[block]
    big = flag_ref[0]
    wide = 2 * BLOCK
    count = (hi - lo) // 2

    def wide_step(j, c):
        return body(pl.multiple_of((lo + 2 * j) * BLOCK, BLOCK), wide, c)

    def last_step(j, c):
        return body(pl.multiple_of((lo + 2 * count + j) * BLOCK, BLOCK), BLOCK, c)

    carry = lax.fori_loop(0, count, wide_step, carry)
    return lax.fori_loop(0, (hi - lo) - 2 * count, last_step, carry)


def attend_kernel(lo_ref, hi_ref, flag_ref, q_ref, k_ref, v_ref, o_ref, lse_ref, vt_ref):
    block = pl.program_id(0)
    group = q_ref.shape[-1]
    heads = group // HEAD_DIM

    @pl.when(block == 0)
    def _():
        for at in range(0, v_ref.shape[1], BLOCK):
            vt_ref[:, at : at + BLOCK] = v_ref[0, at : at + BLOCK, :].T

    query = q_ref[0] * SCALE
    masked = [only_head(query, head, 1).astype(bf16) for head in range(heads)]

    def body(start, size, carry):
        keys = k_ref[0, pl.ds(start, size), :]
        result = []
        for head in range(heads):
            top, total, acc = carry[head]
            scores = (
                lax.dot_general(
                    keys, masked[head], (((1,), (1,)), ((), ())), preferred_element_type=f32
                )
                * LOG2E
            )
            new_top = jnp.maximum(top, jnp.max(scores, axis=0, keepdims=True))
            weight = jnp.exp2(scores - new_top)
            shrink = jnp.exp2(top - new_top)
            total = total * shrink + jnp.sum(weight, axis=0, keepdims=True)
            values = vt_ref[head * HEAD_DIM : (head + 1) * HEAD_DIM, pl.ds(start, size)]
            acc = acc * shrink + jnp.dot(values, weight.astype(bf16), preferred_element_type=f32)
            result.append((new_top, total, acc))
        return tuple(result)

    start = tuple(
        (
            jnp.full((1, BLOCK), -1e30, f32),
            jnp.zeros((1, BLOCK), f32),
            jnp.zeros((HEAD_DIM, BLOCK), f32),
        )
        for _ in range(heads)
    )
    final = key_loop(lo_ref, hi_ref, flag_ref, block, body, start)
    for head in range(heads):
        top, total, acc = final[head]
        o_ref[0, head * HEAD_DIM : (head + 1) * HEAD_DIM, :] = (acc / total).astype(bf16)
        lse_ref[0, head : head + 1, :] = top + jnp.log2(total)


def attend(lo, hi, flag, qkv, out_order):
    _, length, group = qkv.shape
    blocks = length // BLOCK
    return pl.pallas_call(
        attend_kernel,
        grid_spec=pltpu.PrefetchScalarGridSpec(
            num_scalar_prefetch=3,
            grid=(blocks,),
            in_specs=[
                pl.BlockSpec((1, BLOCK, group), lambda i, *s: (0, i, 0)),
                pl.BlockSpec((1, length, group), lambda i, *s: (1, 0, 0)),
                pl.BlockSpec((1, length, group), lambda i, *s: (2, 0, 0)),
            ],
            out_specs=[
                pl.BlockSpec((1, group, BLOCK), lambda i, *s: (out_order(i), 0, 0)),
                pl.BlockSpec((1, 8, BLOCK), lambda i, *s: (i, 0, 0)),
            ],
            scratch_shapes=[pltpu.VMEM((group, length), bf16)],
        ),
        out_shape=[
            jax.ShapeDtypeStruct((blocks, group, BLOCK), bf16),
            jax.ShapeDtypeStruct((blocks, 8, BLOCK), f32),
        ],
        name="attend",
    )(lo, hi, flag, qkv, qkv, qkv)


def attend_back_kernel(
    lo_ref,
    hi_ref,
    flag_ref,
    q_ref,
    k_ref,
    v_ref,
    o_ref,
    do_ref,
    lse_ref,
    cos_ref,
    sin_ref,
    out_ref,
    kt_ref,
    dk_ref,
    dv_ref,
):
    block = pl.program_id(0)
    length = k_ref.shape[1]
    group = q_ref.shape[-1]
    heads = group // HEAD_DIM

    @pl.when(block == 0)
    def _():
        dk_ref[...] = jnp.zeros_like(dk_ref)
        dv_ref[...] = jnp.zeros_like(dv_ref)
        for at in range(0, length, BLOCK):
            kt_ref[:, at : at + BLOCK] = k_ref[0, at : at + BLOCK, :].T

    query = q_ref[0] * SCALE
    grad_t = do_ref[0]
    grad = grad_t.T
    mixed = grad_t.astype(f32) * o_ref[0].astype(f32)
    query_m = jnp.concatenate([only_head(query, h, 1).astype(bf16) for h in range(heads)], axis=0)
    grad_m = jnp.concatenate([only_head(grad, h, 1).astype(bf16) for h in range(heads)], axis=0)
    grad_tm = [only_head(grad_t, h, 0).astype(bf16) for h in range(heads)]
    centre = [
        jnp.sum(mixed[h * HEAD_DIM : (h + 1) * HEAD_DIM], axis=0, keepdims=True)
        for h in range(heads)
    ]
    level = [lse_ref[0, h : h + 1, :] for h in range(heads)]

    def body(start, size, carry):
        keys = k_ref[0, pl.ds(start, size), :]
        values = v_ref[0, pl.ds(start, size), :]
        probs, grads, result = [], [], []
        for head in range(heads):
            rows = slice(head * BLOCK, (head + 1) * BLOCK)
            scores = lax.dot_general(
                keys, query_m[rows], (((1,), (1,)), ((), ())), preferred_element_type=f32
            )
            prob = jnp.exp2(scores * LOG2E - level[head])
            grad_prob = jnp.dot(values, grad_tm[head], preferred_element_type=f32)
            grad_score = (prob * (grad_prob - centre[head])).astype(bf16)
            probs.append(prob.astype(bf16))
            grads.append(grad_score)
            keys_t = kt_ref[head * HEAD_DIM : (head + 1) * HEAD_DIM, pl.ds(start, size)]
            result.append(
                carry[head] + jnp.dot(keys_t, grad_score, preferred_element_type=f32)
            )
        dv_ref[pl.ds(start, size), :] += jnp.dot(
            jnp.concatenate(probs, axis=1), grad_m, preferred_element_type=f32
        )
        dk_ref[pl.ds(start, size), :] += jnp.dot(
            jnp.concatenate(grads, axis=1), query_m, preferred_element_type=f32
        )
        return tuple(result)

    begin = tuple(jnp.zeros((HEAD_DIM, BLOCK), f32) for _ in range(heads))
    final = key_loop(lo_ref, hi_ref, flag_ref, block, body, begin)
    grad_query = (jnp.concatenate(final, axis=0) * SCALE).T
    here = pl.ds(pl.multiple_of(block * BLOCK, BLOCK), BLOCK)
    cosine, sine = cos_ref[here, :], sin_ref[here, :]
    out_ref[0, here, :] = (grad_query * cosine - turn(grad_query) * sine).astype(bf16)

    @pl.when(block == pl.num_programs(0) - 1)
    def _():
        for at in range(0, length, BLOCK):
            part = slice(at, at + BLOCK)
            grad_key = dk_ref[part, :]
            out_ref[1, part, :] = (
                grad_key * cos_ref[part, :] - turn(grad_key) * sin_ref[part, :]
            ).astype(bf16)
            out_ref[2, part, :] = dv_ref[part, :].astype(bf16)


def attend_back(lo, hi, flag, qkv, mixed, grad_mixed, level, cosine, sine, out_order):
    _, length, group = qkv.shape
    blocks = length // BLOCK
    whole = lambda i, *s: (0, 0)
    return pl.pallas_call(
        attend_back_kernel,
        grid_spec=pltpu.PrefetchScalarGridSpec(
            num_scalar_prefetch=3,
            grid=(blocks,),
            in_specs=[
                pl.BlockSpec((1, BLOCK, group), lambda i, *s: (0, i, 0)),
                pl.BlockSpec((1, length, group), lambda i, *s: (1, 0, 0)),
                pl.BlockSpec((1, length, group), lambda i, *s: (2, 0, 0)),
                pl.BlockSpec((1, group, BLOCK), lambda i, *s: (out_order(i), 0, 0)),
                pl.BlockSpec((1, group, BLOCK), lambda i, *s: (out_order(i), 0, 0)),
                pl.BlockSpec((1, 8, BLOCK), lambda i, *s: (i, 0, 0)),
                pl.BlockSpec((length, group), whole),
                pl.BlockSpec((length, group), whole),
            ],
            out_specs=pl.BlockSpec((3, length, group), lambda i, *s: (0, 0, 0)),
            scratch_shapes=[
                pltpu.VMEM((group, length), bf16),
                pltpu.VMEM((length, group), f32),
                pltpu.VMEM((length, group), f32),
            ],
        ),
        out_shape=jax.ShapeDtypeStruct((3, length, group), bf16),
        name="attend_back",
    )(lo, hi, flag, qkv, qkv, qkv, mixed, grad_mixed, level, cosine, sine)


def mm(left, right, contract_left, contract_right):
    return lax.dot_general(
        left,
        right,
        (((contract_left,), (contract_right,)), ((), ())),
        preferred_element_type=f32,
    )


def swap(value):
    return lax.ppermute(value, "frames", [(0, 1), (1, 0)])


def local(
    tokens,
    cotangent,
    bucket,
    clip_of_frame,
    noise_index,
    noise_table,
    w_mod,
    b_mod,
    w_qkv,
    w_out,
    w_up,
    w_down,
):
    tz = lax.axis_size("tensor")
    nb = lax.axis_size("batch")
    z = lax.axis_index("tensor")
    f = lax.axis_index("frames")
    b = lax.axis_index("batch")
    rows, width = tokens.shape[2], tokens.shape[3]
    shard_rows = rows * tz
    length = 2 * shard_rows
    width_local = w_qkv.shape[2]
    group = width_local // 2
    frame_slots = clip_of_frame.shape[1]
    hidden_local = w_up.shape[1]
    half = hidden_local // 2
    quarter = half // nb
    blocks = length // BLOCK

    tokens_local = tokens[0, 0]
    grad_out_local = cotangent[0, 0]

    unit = jnp.where(bucket[0] == 0, FRAME_SMALL // BLOCK, FRAME_LARGE // BLOCK).astype(jnp.int32)
    block_index = jnp.arange(blocks, dtype=jnp.int32)
    block_frame = block_index // unit
    clip_row = clip_of_frame[0]
    frame_ids = jnp.arange(frame_slots, dtype=jnp.int32)
    frame_clip = jnp.sum(
        jnp.where(block_frame[:, None] == frame_ids[None, :], clip_row[None, :], 0), axis=1
    )
    first_block = jnp.min(
        jnp.where(
            frame_clip[:, None] == frame_clip[None, :], block_index[None, :], jnp.int32(blocks)
        ),
        axis=1,
    )
    lo = first_block.astype(jnp.int32)
    hi = ((block_frame + 1) * unit).astype(jnp.int32)
    flag = bucket.astype(jnp.int32)

    all_bucket = lax.all_gather(
        jnp.concatenate([bucket, noise_index[0]]).astype(jnp.int32), "batch", axis=0
    )
    levels = jnp.take(noise_table, all_bucket[:, 1:].reshape(-1), axis=0)
    cond_all = jax.nn.silu(levels).astype(bf16).reshape(nb, frame_slots, width)
    cond = jax.nn.silu(jnp.take(noise_table, noise_index[0], axis=0)).astype(bf16)
    mod_part = jnp.dot(cond, w_mod, preferred_element_type=f32) + b_mod.astype(f32)[None, :]

    tokens_all = lax.all_gather(tokens_local, "tensor", axis=0, tiled=True)
    mod_whole = lax.all_gather(mod_part, "tensor", axis=1, tiled=True)

    own_frames = lax.dynamic_slice(block_frame, (f * tz,), (tz,))
    local_frame = lax.dynamic_index_in_dim(own_frames, z, keepdims=False)
    mod_row = lax.dynamic_slice(mod_whole, (local_frame, 0), (1, 6 * width))
    part = lambda at: mod_row[:, at * width : (at + 1) * width]
    shift_one, scale_one, gate_one, shift_two, scale_two, gate_two = map(part, range(6))

    w_pair = w_qkv.reshape(width, 3, 2, group)
    mine = lax.dynamic_index_in_dim(w_pair, f, axis=2, keepdims=False)
    theirs = lax.dynamic_index_in_dim(w_pair, 1 - f, axis=2, keepdims=False)
    w_arranged = jnp.concatenate(
        [mine.reshape(width, 3 * group), theirs.reshape(width, 3 * group)], axis=1
    )

    start = f * half + b * quarter
    up_piece = lax.dynamic_slice(w_up.T, (start, 0), (quarter, width))
    down_piece = lax.dynamic_slice(w_down, (start, 0), (quarter, width))
    pieces = jnp.stack([up_piece, down_piece])
    gathered = lax.all_gather(pieces, ("batch", "tensor"), axis=1, tiled=True)
    up_t, down = gathered[0], gathered[1]
    out_whole = lax.all_gather(w_out, "tensor", axis=0, tiled=True)

    cos_all, sin_all = rotary_tables(jnp.arange(length, dtype=jnp.int32), group)
    cos_own = lax.dynamic_slice(cos_all, (f * shard_rows, 0), (shard_rows, group))
    sin_own = lax.dynamic_slice(sin_all, (f * shard_rows, 0), (shard_rows, group))
    attn_in, qkv_pair = project(
        own_frames, tokens_all, mod_whole[:, : 2 * width], w_arranged, cos_own, sin_own
    )
    received = swap(qkv_pair[1])
    kept = qkv_pair[0]
    is_first = f == 0
    qkv = jnp.concatenate(
        [jnp.where(is_first, kept, received), jnp.where(is_first, received, kept)], axis=1
    )

    out_order = lambda i: (i % tz) * 2 + i // tz
    mixed, level = attend(lo, hi, flag, qkv, out_order)
    attn_t = lax.all_to_all(mixed, ("tensor", "frames"), 0, 0, tiled=True).reshape(width, rows)
    branch_one = mm(attn_t, out_whole, 0, 0)

    residual = tokens_local.astype(f32)
    normed_one, inverse_one = normalize(residual)
    mixed_one = residual + gate_one * branch_one
    normed_two, inverse_two = normalize(mixed_one)
    mlp_in = (normed_two * (1.0 + scale_two) + shift_two).astype(bf16)
    mlp_rows = jnp.concatenate([mlp_in, swap(mlp_in)], axis=0)
    grad_out = grad_out_local.astype(f32)
    grad_branch_two = (gate_two * grad_out).astype(bf16)
    grad_two_rows = jnp.concatenate([grad_branch_two, swap(grad_branch_two)], axis=0)

    pre = mm(mlp_rows, up_t, 1, 1)
    grad_hidden = mm(grad_two_rows, down, 1, 1)
    hidden_f32, gelu_pull = jax.vjp(lambda v: jax.nn.gelu(v, approximate=True), pre)
    hidden = hidden_f32.astype(bf16)
    grad_pre = gelu_pull(grad_hidden)[0].astype(bf16)
    grad_mlp_rows = mm(grad_pre, up_t, 1, 0)
    grad_mlp_in = grad_mlp_rows[:rows] + swap(grad_mlp_rows[rows:])
    branch_two_rows = mm(hidden, down, 1, 0)
    branch_two = branch_two_rows[:rows] + swap(branch_two_rows[rows:])
    result = (mixed_one + gate_two * branch_two).astype(bf16)
    grad_gate_two = grad_out * branch_two

    grad_down = mm(hidden, grad_two_rows, 0, 0).astype(bf16)
    grad_up_t = mm(grad_pre, mlp_rows, 0, 0).astype(bf16)

    grad_scale_two = grad_mlp_in * normed_two
    grad_mixed_one = grad_out + norm_back(grad_mlp_in * (1.0 + scale_two), normed_two, inverse_two)
    grad_branch_one = (gate_one * grad_mixed_one).astype(bf16)
    grad_gate_one = grad_mixed_one * branch_one

    grad_attn_t = mm(out_whole, grad_branch_one, 1, 1).astype(bf16)
    grad_mixed = lax.all_to_all(
        grad_attn_t.reshape(blocks, group, rows), ("tensor", "frames"), 0, 0, tiled=True
    )
    grad_out_weights = mm(attn_t, grad_branch_one, 1, 0).astype(bf16)

    grad_qkv = attend_back(
        lo, hi, flag, qkv, mixed, grad_mixed, level, cos_all, sin_all, out_order
    )
    grad_first, grad_second = grad_qkv[:, :shard_rows], grad_qkv[:, shard_rows:]
    grad_received = swap(jnp.where(is_first, grad_second, grad_first))
    grad_kept = jnp.where(is_first, grad_first, grad_second)
    grad_arranged = jnp.concatenate(
        [grad_kept[0], grad_kept[1], grad_kept[2]]
        + [grad_received[0], grad_received[1], grad_received[2]],
        axis=1,
    )
    grad_attn_part = mm(grad_arranged, w_arranged, 1, 1)

    normed_all, _ = normalize(tokens_all.astype(f32))
    blocked = grad_attn_part.reshape(tz, rows, width)
    sum_shift_one = jnp.sum(blocked, axis=1)
    sum_scale_one = jnp.sum(blocked * normed_all.reshape(tz, rows, width), axis=1)
    local_sums = jnp.concatenate(
        [
            jnp.sum(v, axis=0)
            for v in (grad_gate_one, grad_mlp_in, grad_scale_two, grad_gate_two)
        ]
    )
    own_slot = (jnp.arange(tz, dtype=jnp.int32) == z).astype(f32)
    frame_sums = jnp.concatenate(
        [sum_shift_one, sum_scale_one, own_slot[:, None] * local_sums[None, :]], axis=1
    )
    share = lax.psum_scatter(frame_sums, "tensor", scatter_dimension=1, tiled=True)
    shares = lax.all_gather(share, ("batch", "frames"), axis=0, tiled=True)
    all_unit = jnp.where(
        all_bucket[:, 0] == 0, FRAME_SMALL // BLOCK, FRAME_LARGE // BLOCK
    ).astype(jnp.int32)
    all_frame = block_index[None, :] // all_unit[:, None]
    picked = (all_frame[:, :, None] == frame_ids[None, None, :]).astype(f32)
    cond_blocks = jnp.einsum("bif,bfd->bid", picked, cond_all.astype(f32), precision=highest)
    grad_w_mod = mm_highest(cond_blocks.reshape(nb * blocks, width), shares)
    grad_b_mod = jnp.sum(shares, axis=0)

    grad_attn_in = lax.psum_scatter(
        grad_attn_part.astype(bf16), "tensor", scatter_dimension=0, tiled=True
    ).astype(f32)
    grad_tokens = grad_mixed_one + norm_back(
        grad_attn_in * (1.0 + scale_one), normed_one, inverse_one
    )

    grad_w_arranged = mm(attn_in, grad_arranged, 0, 0)
    mine_grad = grad_w_arranged[:, : 3 * group].reshape(width, 3, 1, group)
    theirs_grad = grad_w_arranged[:, 3 * group :].reshape(width, 3, 1, group)
    grad_w_qkv = jnp.concatenate(
        [
            jnp.where(is_first, mine_grad, theirs_grad),
            jnp.where(is_first, theirs_grad, mine_grad),
        ],
        axis=2,
    ).reshape(width, 3, width_local)
    grad_w_qkv = lax.psum(grad_w_qkv.astype(bf16), ("frames", "batch")).astype(f32)
    grad_w_out = lax.psum(
        lax.psum_scatter(grad_out_weights, "tensor", scatter_dimension=0, tiled=True),
        ("frames", "batch"),
    ).astype(f32)

    def reduce_rows(grad):
        shard = lax.psum_scatter(grad, ("batch", "tensor"), scatter_dimension=0, tiled=True)
        return lax.all_gather(shard, ("frames", "batch"), axis=0, tiled=True).astype(f32)

    grad_w_down = reduce_rows(grad_down)
    grad_w_up = reduce_rows(grad_up_t).T
    return (
        result.reshape(1, 1, rows, width),
        grad_tokens.astype(bf16).reshape(1, 1, rows, width),
        grad_w_mod,
        grad_b_mod,
        grad_w_qkv,
        grad_w_out,
        grad_w_up,
        grad_w_down,
    )


def mm_highest(left, right):
    return lax.dot_general(left, right, (((0,), (0,)), ((), ())), precision=highest)


def solution(mesh):
    placed = (
        P("batch", "frames", "tensor", None),
        P("batch", "frames", "tensor", None),
        P("batch"),
        P("batch", None),
        P("batch", None),
        P(),
        P(None, "tensor"),
        P("tensor"),
        P(None, None, "tensor"),
        P("tensor", None),
        P(None, "tensor"),
        P("tensor", None),
    )
    return jax.shard_map(
        local,
        mesh=mesh,
        in_specs=placed,
        out_specs=(
            P("batch", "frames", "tensor", None),
            P("batch", "frames", "tensor", None),
            P(None, "tensor"),
            P("tensor"),
            P(None, None, "tensor"),
            P("tensor", None),
            P(None, "tensor"),
            P("tensor", None),
        ),
        check_vma=False,
    )
```

time: 991 us -> 755 us (0.76)
  waiting for transfers between devices: 623 us -> 479 us
  matrix products: 156 us -> 53 us
  Pallas kernels: 0 us -> 66.1 us
  other arithmetic: 102 us -> 37.5 us
  starting transfers between devices: 7.66 us -> 20 us
    reduce_scatter x5 -> x4, waiting for transfers between devices: 298 us -> 180 us  [the longest x2 139 us: reduce_rows(): lax.psum_scatter(grad, ('batch', 'tensor'), scatter_dimension=0, tiled=True)]
    dot_general x30 -> x14, matrix products: 156 us -> 53 us  [the longest x11 45.2 us: mm(): lax.dot_general(left, right, (((contract_left,), (contract_right,)), ((),...]
    psum x1, waiting for transfers between devices: 121 us -> 46.6 us  [local(): lax.psum(grad_w_qkv.astype(bf16), ('frames', 'batch')).astype(f32)]
    pallas_call x0 -> x3, Pallas kernels: none -> 66.1 us  [the longest x1 31.6 us: attend_back(): pl.pallas_call(attend_back_kernel, grid_spec=pltpu.PrefetchScalarGridSpec...]
    unnamed x12, waiting for transfers between devices: 1.35 us -> 52.4 us
    convert_element_type x16 -> x8, other arithmetic: 50 us -> 8.95 us  [the longest x1 4.07 us: reduce_rows(): lax.all_gather(shard, ('frames', 'batch'), axis=0, tiled=True).astype(f32)]
    all_gather x6 -> x5, waiting for transfers between devices: 202 us -> 164 us  [the longest x1 106 us: local(): gathered = lax.all_gather(pieces, ('batch', 'tensor'), axis=1, tiled=True)]
    all_to_all x0 -> x2, waiting for transfers between devices: none -> 30.1 us  [the longest x1 18 us: local(): lax.all_to_all(grad_attn_t.reshape(blocks, group, rows), ('tensor', 'fram...]
  transfers between devices with their start and end apart: 16 -> 19, of which waited for: 11 -> 15; matrix products, arithmetic and copies ran while one was open for 20% -> 15% of each run, Pallas kernels for 0% -> 9%
where the time goes in v1:
time: 755 us; the launch traced here: 744 us
  waiting for transfers between devices  479 us (63%)
  Pallas kernels  66.1 us (9%)
  matrix products  53 us (7%)
  local copies, waits for them, and re-layouts  38.1 us (5%)
  other arithmetic  37.5 us (5%)
  blocking collectives  32.8 us (4%)
  starting transfers between devices  20 us (3%)
  between operations  18 us (2%)
    reduce_scatter x2, waiting for transfers between devices, reduce_rows(): lax.psum_scatter(grad, ('batch', 'tensor'), scatter_dimension=0, tiled=True)  139 us
    all_gather x1, waiting for transfers between devices, local(): gathered = lax.all_gather(pieces, ('batch', 'tensor'), axis=1, tiled=True)  106 us
    unnamed x12, waiting for transfers between devices  52.4 us
    psum x1, waiting for transfers between devices, local(): lax.psum(grad_w_qkv.astype(bf16), ('frames', 'batch')).astype(f32)  46.6 us
    dot_general x11, matrix products, mm(): lax.dot_general(left, right, (((contract_left,), (contract_right,)), ((),...  45.2 us
    all_gather x2, waiting for transfers between devices, reduce_rows(): lax.all_gather(shard, ('frames', 'batch'), axis=0, tiled=True).astype(f32)  45.2 us
    reduce_scatter x1, waiting for transfers between devices, local(): lax.psum_scatter(grad_attn_part.astype(bf16), 'tensor', scatter_dimension...  41.1 us
    pallas_call x1, Pallas kernels, attend_back(): pl.pallas_call(attend_back_kernel, grid_spec=pltpu.PrefetchScalarGridSpec...  31.6 us
  transfers between devices with their start and end apart: 19, of which 15 were waited for; matrix products, arithmetic and copies ran while one was open for 15% of the time, Pallas kernels for 9%

profile of v1, /device:TPU:0, one launch (start us, length us, event | category | flops | bytes accessed | tf_op | source)
XLA Modules:
  0.0 744.2 jit_solution(8338408421990341562)
XLA Ops:
  11.5 1.8 pad_maximum_fusion.11
  14.1 2.7 gather_fusion
  17.4 16.8 %all_gather.27 = f32[8,6144]{1,0:T(8,128)S(1)} all-gather(f32[8,1536]{1,0:T(8,128)S(1)} %convolution_add_fusion), channel_id=1, replica_groups=mesh['tensor'=4,'frames'=2,'batch'=4] {'tensor'}, dimensions={1}, use_global_device_ids=true | all-gather | bytes 245760 | tf_op jit(solution)/shard_map/all_gather | solution.py:399
  34.9 1.7 copy.52
  39.9 3.7 fusion.33
  43.6 1.7 pad_maximum_fusion.3
  48.4 12.8 %all-gather.17.cloned.1.call-done = bf16[1,1,1024,1024]{3,2,1,0:T(8,128)(2,1)} async-done(((bf16[1,1,256,1024]{3,2,1,0:T(8,128)(2,1)}), bf16[1,1,1024,1024]{3,2,1,0:T(8,128)(2,1)}) %all-gather.17.cloned.1.call-update) | async-done | bytes 2097168 | tf_op jit(solution)/shard_map/all_gather | solution.py:398
  61.2 7.6 %project.1 = (bf16[1024,1024]{1,0:T(8,128)(2,1)}, bf16[2,3,1024,128]{3,2,1,0:T(8,128)(2,1)}) custom-call(s32[4]{0:T(128)} %dynamic_slice.34.frame_ref, bf16[1024,1024]{1,0:T(8,128)(2,1)} %bitcast.148, f32[8,2048]{1,0:T(8,128)} %slice.108.mod_ref, bf16[1024,768]{1,0:T(8,128)(2,1)} %pad_maximum_fusion.w_ref, f32[1024,128]{1,0:T(8,128)} %constant_dynamic-slice_fusion.2.cos_ref, ...), custom_call_target="tpu_custom_call" | custom-call | tf_op jit(solution)/shard_map/project/pallas_call | solution.py:88
  74.9 26.8 %attend.1 = (bf16[8,128,256]{2,1,0:T(8,128)(2,1)}, f32[8,8,256]{2,1,0:T(8,128)}) custom-call(s32[8]{0:T(128)} %select_reduce_fusion.lo_ref, s32[8]{0:T(128)} %add_multiply_fusion.hi_ref, s32[1]{0:T(128)S(6)} %copy.71.flag_ref, bf16[3,2048,128]{2,1,0:T(8,128)(2,1)} %pad_maximum_fusion.1.q_ref.k_ref.v_ref, ...), custom_call_target="tpu_custom_call" | custom-call | tf_op jit(solution)/shard_map/attend/pallas_call | solution.py:185
  101.7 3.5 all-to-all-start
  108.4 12.1 %all-to-all-done = bf16[8,128,256]{2,1,0:T(8,128)(2,1)S(1)} async-done(((bf16[8,128,256]{2,1,0:T(8,128)(2,1)}), bf16[8,128,256]{2,1,0:T(8,128)(2,1)S(1)}, u32[]{:S(2)}, u32[]{:S(2)}) %all-to-all-start) | async-done | bytes 524320 | tf_op jit(solution)/shard_map/all_to_all | solution.py:437
  120.4 3.4 fusion.60
  126.5 106.2 %all-gather.11.cloned.1.call-done = bf16[2,2048,1024]{2,1,0:T(8,128)(2,1)} async-done(((bf16[2,128,1024]{2,1,0:T(8,128)(2,1)}), bf16[2,2048,1024]{2,1,0:T(8,128)(2,1)}) %all-gather.11.cloned.1.call-update) | async-done | bytes 8388624 | tf_op jit(solution)/shard_map/all_gather | solution.py:418
  232.7 4.9 fusion.12
  237.6 6.2 fusion.9
  245.1 2.3 fusion.11
  247.7 2.7 fusion.14
  254.8 2.0 convolution_convert_fusion.2
  256.9 6.1 convolution_convert_fusion.1
  263.0 10.2 %reduce-scatter.14.cloned.1.call-start = ((), (), s32[]{:S(2)}) async-start(), calls=%async_computation.13 | async-start | bytes 4456448 | tf_op jit(solution)/shard_map/reduce_scatter | solution.py:538
  273.3 7.3 convolution_convert_fusion
  280.6 3.3 fusion.19
  283.9 2.0 copy.57
  285.9 4.1 all-to-all-start.1
  291.2 18.0 %all-to-all-done.1.do_ref = bf16[8,128,256]{2,1,0:T(8,128)(2,1)} async-done(((bf16[8,128,256]{2,1,0:T(8,128)(2,1)}), bf16[8,128,256]{2,1,0:T(8,128)(2,1)}, u32[]{:S(2)}, u32[]{:S(2)}) %all-to-all-start.1) | async-done | bytes 524320 | tf_op jit(solution)/shard_map/all_to_all | solution.py:471
  309.2 31.6 %attend_back.1 = bf16[3,2048,128]{2,1,0:T(8,128)(2,1)} custom-call(s32[8]{0:T(128)} %select_reduce_fusion.lo_ref, s32[8]{0:T(128)} %add_multiply_fusion.hi_ref, s32[1]{0:T(128)S(6)} %copy.71.flag_ref, bf16[3,2048,128]{2,1,0:T(8,128)(2,1)} %pad_maximum_fusion.1.q_ref.k_ref.v_ref, bf16[3,2048,128]{2,1,0:T(8,128)(2,1)} %pad_maximum_fusion.1.q_ref.k_ref.v_ref, ...), custom_call_target="tpu_custom_call" | custom-call | tf_op jit(solution)/shard_map/attend_back/pallas_call | solution.py:299
  342.9 1.9 collective-permute-done.5
  345.0 3.1 fusion.62
  349.4 2.2 copy.60
  351.6 3.9 fusion.64
  355.8 2.9 copy.58
  358.8 3.8 convert_element_type.128
  363.3 40.3 %reduce-scatter.12.cloned.1.call-done = bf16[128,1024]{1,0:T(8,128)(2,1)} async-done(((bf16[2048,1024]{1,0:T(8,128)(2,1)}), bf16[128,1024]{1,0:T(8,128)(2,1)}) %reduce-scatter.12.cloned.1.call-update) | async-done | bytes 262160 | tf_op jit(solution)/shard_map/reduce_scatter | solution.py:538
  403.7 98.6 %reduce-scatter.14.cloned.1.call-done = bf16[128,1024]{1,0:T(8,128)(2,1)} async-done(((bf16[2048,1024]{1,0:T(8,128)(2,1)}), bf16[128,1024]{1,0:T(8,128)(2,1)}) %reduce-scatter.14.cloned.1.call-update) | async-done | bytes 262160 | tf_op jit(solution)/shard_map/reduce_scatter | solution.py:538
  503.7 6.5 all-reduce
  510.5 2.8 gather_fusion.1
  514.0 50.2 %reduce-scatter.16.cloned.1.call-done = f32[1536,4]{1,0:T(8,128)} async-done(((f32[6144,4]{1,0:T(8,128)}), f32[1536,4]{1,0:T(8,128)}) %reduce-scatter.16.cloned.1.call-update) | async-done | bytes 24592
  565.6 9.5 %all-gather.2 = f32[8,4,1536]{2,1,0:T(4,128)S(1)} all-gather(f32[1,4,1536]{2,1,0:T(4,128)S(1)} %bitcast.163), channel_id=1, replica_groups=mesh['tensor'=4,'frames'=2,'batch'=4] {'batch','frames'}, dimensions={0}, use_global_device_ids=true | all-gather | bytes 221184 | tf_op jit(solution)/shard_map/all_gather | solution.py:504
  575.8 7.0 fusion.63
  582.8 46.6 %all-reduce.4.cloned.1.call-done = (bf16[1024,3,256]{2,0,1:T(8,128)(2,1)}, bf16[256,1024]{1,0:T(8,128)(2,1)}) async-done(((bf16[1024,3,256]{2,0,1:T(8,128)(2,1)}, bf16[256,1024]{1,0:T(8,128)(2,1)}), (bf16[1024,3,256]{2,0,1:T(8,128)(2,1)}, bf16[256,1024]{1,0:T(8,128)(2,1)})) %all-reduce.4.cloned.1.call-update) | async-done | bytes 2097168 | tf_op jit(solution)/shard_map/psum | solution.py:531
  629.3 3.4 convert_element_type.129
  633.9 41.1 %reduce-scatter.8.cloned.1.call-done = bf16[256,1024]{1,0:T(8,128)(2,1)} async-done(((bf16[1024,1024]{1,0:T(8,128)(2,1)}), bf16[256,1024]{1,0:T(8,128)(2,1)}) %reduce-scatter.8.cloned.1.call-update) | async-done | bytes 524304 | tf_op jit(solution)/shard_map/reduce_scatter | solution.py:514
  676.4 2.3 fusion.32
  678.6 25.0 %all-gather.13.cloned.1.call-done = bf16[1024,1024]{1,0:T(8,128)(2,1)} async-done(((bf16[128,1024]{1,0:T(8,128)(2,1)}), bf16[1024,1024]{1,0:T(8,128)(2,1)}) %all-gather.13.cloned.1.call-update) | async-done | bytes 2097168 | tf_op jit(solution)/shard_map/all_gather | solution.py:539
  703.7 4.1 convert_bitcast_fusion
  707.7 5.5 copy.59
  713.2 20.1 %all-gather.15.cloned.1.call-done = bf16[1024,1024]{1,0:T(8,128)(2,1)} async-done(((bf16[128,1024]{1,0:T(8,128)(2,1)}), bf16[1024,1024]{1,0:T(8,128)(2,1)}) %all-gather.15.cloned.1.call-update) | async-done | bytes 2097168 | tf_op jit(solution)/shard_map/all_gather | solution.py:539
  733.4 4.1 convert_element_type.134
  (165 shorter events, 39.8 us)
Async XLA Ops:
  7.2 9.7 %copy-start = (bf16[1024,1536]{1,0:T(8,128)(2,1)S(1)}, bf16[1024,1536]{1,0:T(8,128)(2,1)}, u32[]{:S(2)}) copy-start(bf16[1024,1536]{1,0:T(8,128)(2,1)} %param.18) | copy-start | bytes 9437188
  7.2 6.2 copy-start.19
  7.2 6.8 copy-start.20
  7.2 54.0 %all-gather.17.cloned.1.call-start = ((), (), s32[]{:S(2)}) async-start(), calls=%async_computation.15 | async-start | bytes 2621440 | tf_op jit(solution)/shard_map/all_gather | solution.py:398
  7.9 100.4 %all-gather.9.cloned.1.call-start = ((), (), s32[]{:S(2)}) async-start(), calls=%async_computation.7 | async-start | bytes 2621440 | tf_op jit(solution)/shard_map/all_gather | solution.py:420
  8.7 224.0 %all-gather.11.cloned.1.call-start = ((), (), s32[]{:S(2)}) async-start(), calls=%async_computation.8 | async-start | bytes 8912896 | tf_op jit(solution)/shard_map/all_gather | solution.py:418
  43.6 3.5 copy-start.8
  43.6 3.5 copy-start.10
  45.3 23.5 %copy-start.5 = (f32[2048,128]{1,0:T(8,128)}, f32[2048,128]{1,0:T(8,128)S(1)}, u32[]{:S(2)}) copy-start(f32[2048,128]{1,0:T(8,128)S(1)} %get-tuple-element.105.cos_ref) | copy-start | bytes 3145732
  45.3 23.4 %copy-start.6 = (f32[2048,128]{1,0:T(8,128)}, f32[2048,128]{1,0:T(8,128)S(1)}, u32[]{:S(2)}) copy-start(f32[2048,128]{1,0:T(8,128)S(1)} %get-tuple-element.106.sin_ref) | copy-start | bytes 3145732
  61.2 9.6 %copy-start.22 = (s32[1,8]{1,0:T(1,128)S(1)}, s32[1,8]{1,0:T(1,128)}, u32[]{:S(2)}) copy-start(s32[1,8]{1,0:T(1,128)} %param.15) | copy-start | bytes 100
  70.0 2.4 collective-permute-start
  74.9 33.3 %copy-start.3 = (bf16[1,1,256,1024]{3,2,1,0:T(8,128)(2,1)S(1)}, bf16[1,1,256,1024]{3,2,1,0:T(8,128)(2,1)}, u32[]{:S(2)}) copy-start(bf16[1,1,256,1024]{3,2,1,0:T(8,128)(2,1)} %param.12) | copy-start | bytes 1572868
  101.7 18.8 %all-to-all-start = ((bf16[8,128,256]{2,1,0:T(8,128)(2,1)}), bf16[8,128,256]{2,1,0:T(8,128)(2,1)S(1)}, u32[]{:S(2)}, u32[]{:S(2)}) async-start(bf16[8,128,256]{2,1,0:T(8,128)(2,1)} %get-tuple-element.13.o_ref), calls=%async_computation | async-start | bytes 1048576 | tf_op jit(solution)/shard_map/all_to_all | solution.py:437
  105.2 257.3 %reduce-scatter.10.cloned.1.call-start = ((), (), s32[]{:S(2)}) async-start(), calls=%async_computation.10 | async-start | bytes 2621440 | tf_op jit(solution)/shard_map/reduce_scatter | solution.py:533
  120.4 4.0 copy-start.12
  124.4 113.2 %copy-start.16 = (bf16[256,1024]{1,0:T(8,128)(2,1)}, bf16[256,1024]{1,0:T(8,128)(2,1)S(1)}, u32[]{:S(2)}) copy-start(bf16[256,1024]{1,0:T(8,128)(2,1)S(1)} %add_convert_fusion.1) | copy-start | bytes 1572868
  124.4 2.1 collective-permute-start.1
  124.6 113.0 %copy-start.14 = (bf16[256,1024]{1,0:T(8,128)(2,1)}, bf16[256,1024]{1,0:T(8,128)(2,1)S(1)}, u32[]{:S(2)}) copy-start(bf16[256,1024]{1,0:T(8,128)(2,1)S(1)} %fusion.28) | copy-start | bytes 1572868
  124.6 113.0 %collective-permute-start.3 = (bf16[256,1024]{1,0:T(8,128)(2,1)S(1)}, bf16[256,1024]{1,0:T(8,128)(2,1)}, u32[]{:S(2)}, u32[]{:S(2)}) collective-permute-start(bf16[256,1024]{1,0:T(8,128)(2,1)S(1)} %fusion.28), channel_id=1, source_target_pairs={{0,4},{4,0},{1,5},{5,1},{2,6},{6,2},{3,7},{7,3},{8,12},{12,8},{9,1... | collective-permute-start | bytes 1572872 | tf_op jit(solution)/shard_map/ppermute | solution.py:336
  232.7 4.9 copy-start.21
  237.5 10.1 %copy-start.24 = (f32[512,2048]{1,0:T(8,128)}, f32[512,2048]{1,0:T(8,128)S(1)}, u32[]{:S(2)}) copy-start(f32[512,2048]{1,0:T(8,128)S(1)} %fusion.12) | copy-start | bytes 12582916
  243.8 1.3 copy-start.25
  247.6 3.4 collective-permute-start.4
  250.3 3.0 copy-start.7
  250.5 2.8 collective-permute-start.2
  254.8 2.1 copy-start.17
  256.9 146.7 %reduce-scatter.12.cloned.1.call-start = ((), (), s32[]{:S(2)}) async-start(), calls=%async_computation.11 | async-start | bytes 4456448 | tf_op jit(solution)/shard_map/reduce_scatter | solution.py:538
  263.0 10.2 %copy-start.15 = (bf16[256,1024]{1,0:T(8,128)(2,1)S(1)}, bf16[256,1024]{1,0:T(8,128)(2,1)}, u32[]{:S(2)}) copy-start(bf16[256,1024]{1,0:T(8,128)(2,1)} %copy-done.14) | copy-start | bytes 1572868
  263.0 239.2 %reduce-scatter.14.cloned.1.call-start = ((), (), s32[]{:S(2)}) async-start(), calls=%async_computation.13 | async-start | bytes 4456448 | tf_op jit(solution)/shard_map/reduce_scatter | solution.py:538
  280.6 9.5 %copy-start.2 = (bf16[1,1,1024,1024]{3,2,1,0:T(8,128)(2,1)S(1)}, bf16[1,1,1024,1024]{3,2,1,0:T(8,128)(2,1)}, u32[]{:S(2)}) copy-start(bf16[1,1,1024,1024]{3,2,1,0:T(8,128)(2,1)} %all-gather.17.cloned.1.call-done) | copy-start | bytes 6291460
  285.9 23.3 %all-to-all-start.1 = ((bf16[8,128,256]{2,1,0:T(8,128)(2,1)}), bf16[8,128,256]{2,1,0:T(8,128)(2,1)}, u32[]{:S(2)}, u32[]{:S(2)}) async-start(bf16[8,128,256]{2,1,0:T(8,128)(2,1)} %bitcast.157), calls=%async_computation.1 | async-start | bytes 1048576 | tf_op jit(solution)/shard_map/all_to_all | solution.py:471
  290.1 274.1 %reduce-scatter.16.cloned.1.call-start = ((), (), s32[]{:S(2)}) async-start(), calls=%async_computation.16 | async-start | bytes 3932160
  340.8 4.2 copy-start.9
  340.8 4.2 copy-start.11
  342.4 2.4 collective-permute-start.5
  345.0 3.2 copy-start.18
  355.5 273.8 %all-reduce.4.cloned.1.call-start = ((), (), s32[]{:S(2)}) async-start(), calls=%async_computation.17 | async-start | bytes 4194304 | tf_op jit(solution)/shard_map/psum | solution.py:531
  362.5 139.8 %copy-start.23 = (u32[32]{0:T(128)S(1)}, u32[32]{0:T(128)}, u32[]{:S(2)}) copy-start(u32[32]{0:T(128)} %constant.142) | copy-start | bytes 388
  362.6 312.4 %reduce-scatter.8.cloned.1.call-start = ((), (), s32[]{:S(2)}) async-start(), calls=%async_computation.9 | async-start | bytes 2621440 | tf_op jit(solution)/shard_map/reduce_scatter | solution.py:514
  363.3 340.4 %all-gather.13.cloned.1.call-start = ((), (), s32[]{:S(2)}) async-start(), calls=%async_computation.12 | async-start | bytes 2359296 | tf_op jit(solution)/shard_map/all_gather | solution.py:539
  403.7 329.7 %all-gather.15.cloned.1.call-start = ((), (), s32[]{:S(2)}) async-start(), calls=%async_computation.14 | async-start | bytes 2359296 | tf_op jit(solution)/shard_map/all_gather | solution.py:539
  629.3 3.4 copy-start.13
  629.3 45.6 %copy-start.4 = (bf16[1,1,256,1024]{3,2,1,0:T(8,128)(2,1)S(1)}, bf16[1,1,256,1024]{3,2,1,0:T(8,128)(2,1)}, u32[]{:S(2)}) copy-start(bf16[1,1,256,1024]{3,2,1,0:T(8,128)(2,1)} %param.12) | copy-start | bytes 1572868
  707.7 29.7 %copy-start.1 = (bf16[1024,1536]{1,0:T(8,128)(2,1)S(1)}, bf16[1024,1536]{1,0:T(8,128)(2,1)}, u32[]{:S(2)}) copy-start(bf16[1024,1536]{1,0:T(8,128)(2,1)} %param.18) | copy-start | bytes 9437188
Sparse Core Ops, SparseCore 0:
  9.6 51.5 all-gather.16
  62.7 44.3 all-gather.8
  110.5 122.0 all-gather.10
  257.0 44.3 reduce-scatter.9
  304.1 99.4 reduce-scatter.11
  406.4 95.8 reduce-scatter.13
  505.1 59.0 reduce-scatter.15
  567.5 61.8 all-reduce.3
  632.2 42.6 reduce-scatter.7
  676.7 26.9 all-gather.12
  705.6 27.7 all-gather.14

commit v2 on v1

--- a/solution.py
+++ b/solution.py
@@ -336,6 +336,136 @@
     return lax.ppermute(value, "frames", [(0, 1), (1, 0)])
 
 
+def paired(value, axis, step):
+    count = lax.axis_size(axis)
+    return lax.ppermute(value, axis, [(i, i ^ step) for i in range(count)])
+
+
+def direct():
+    return lax.axis_size("tensor") == 4 and lax.axis_size("batch") == 4
+
+
+def gather_hidden(up_t, down):
+    nb = lax.axis_size("batch")
+    f, b = lax.axis_index("frames"), lax.axis_index("batch")
+    half, width = up_t.shape[0] // 2, up_t.shape[1]
+    quarter = half // nb
+    if not direct():
+        start = (f * half + b * quarter, 0)
+        pieces = jnp.stack(
+            [lax.dynamic_slice(v, start, (quarter, width)) for v in (up_t, down)]
+        )
+        gathered = lax.all_gather(pieces, ("batch", "tensor"), axis=1, tiled=True)
+        return gathered[0], gathered[1]
+
+    def own(values):
+        return [
+            lax.dynamic_slice(values, (f * half + (b ^ r) * quarter, 0), (quarter, width))
+            for r in range(nb)
+        ]
+
+    ups, downs = own(up_t), own(down)
+    piece = jnp.stack([ups[0], downs[0]])
+    arrived = [paired(piece, "tensor", step) for step in (1, 2, 3)]
+    for group in (arrived[:1], arrived[1:]):
+        up = jnp.stack([v[0] for v in group])
+        low = jnp.stack([v[1] for v in group])
+        up_x = paired(up, "batch", 1)
+        low_y = paired(low, "batch", 2)
+        up_far = paired(jnp.stack([up, up_x]), "batch", 2)
+        low_far = paired(jnp.stack([low, low_y]), "batch", 1)
+        for at in range(len(group)):
+            ups += [up[at], up_x[at], up_far[0, at], up_far[1, at]]
+            downs += [low[at], low_far[0, at], low_y[at], low_far[1, at]]
+    return jnp.concatenate(ups, axis=0), jnp.concatenate(downs, axis=0)
+
+
+def collect_rows(partial, rows):
+    z = lax.axis_index("tensor")
+    tz = lax.axis_size("tensor")
+    if tz & (tz - 1):
+        return lax.psum_scatter(partial, "tensor", scatter_dimension=0, tiled=True).astype(f32)
+    block = lambda at: lax.dynamic_slice(partial, (at * rows, 0), (rows, partial.shape[1]))
+    total = block(z).astype(f32)
+    for step in range(tz - 1, 0, -1):
+        total = total + paired(block(z ^ step), "tensor", step).astype(f32)
+    return total
+
+
+def place_kernel(order_ref, up_ref, down_ref, up_out, down_out):
+    up_out[...] = up_ref[0].astype(f32).T
+    down_out[...] = down_ref[0].astype(f32)
+
+
+def place(order, ups, downs):
+    count, quarter, width = ups.shape
+    return pl.pallas_call(
+        place_kernel,
+        grid_spec=pltpu.PrefetchScalarGridSpec(
+            num_scalar_prefetch=1,
+            grid=(count,),
+            in_specs=[pl.BlockSpec((1, quarter, width), lambda i, o: (o[i], 0, 0))] * 2,
+            out_specs=[
+                pl.BlockSpec((width, quarter), lambda i, o: (0, i)),
+                pl.BlockSpec((quarter, width), lambda i, o: (i, 0)),
+            ],
+        ),
+        out_shape=[
+            jax.ShapeDtypeStruct((width, count * quarter), f32),
+            jax.ShapeDtypeStruct((count * quarter, width), f32),
+        ],
+        name="place",
+    )(order, ups, downs)
+
+
+def reduce_hidden(grad_up_t, grad_down):
+    nb = lax.axis_size("batch")
+    f, b = lax.axis_index("frames"), lax.axis_index("batch")
+    width = grad_up_t.shape[1]
+    if not direct():
+
+        def reduce_rows(grad):
+            shard = lax.psum_scatter(grad, ("batch", "tensor"), scatter_dimension=0, tiled=True)
+            return lax.all_gather(shard, ("frames", "batch"), axis=0, tiled=True).astype(f32)
+
+        return reduce_rows(grad_up_t).T, reduce_rows(grad_down)
+    up = grad_up_t.reshape(4, nb, -1, width)
+    down = grad_down.reshape(4, nb, -1, width)
+    added = lambda v, w: (v.astype(f32) + w.astype(f32)).astype(bf16)
+    parts = {}
+    for group in ((2, 3), (0, 1)):
+        at = slice(group[0], group[1] + 1)
+        u, d = up[at], down[at]
+        u_near = added(u[:, :2], paired(u[:, 2:], "batch", 2))
+        d_sent = jnp.stack([d[:, 1], d[:, 3]], axis=1)
+        d_kept = jnp.stack([d[:, 0], d[:, 2]], axis=1)
+        d_near = added(d_kept, paired(d_sent, "batch", 1))
+        u_sum = added(u_near[:, 0], paired(u_near[:, 1], "batch", 1))
+        d_sum = added(d_near[:, 0], paired(d_near[:, 1], "batch", 2))
+        for i, step in enumerate(group):
+            parts[step] = jnp.stack([u_sum[i], d_sum[i]])
+    total = parts[0].astype(f32)
+    for step in (2, 3, 1):
+        total = total + paired(parts[step], "tensor", step).astype(f32)
+    u, d = total[0].astype(bf16), total[1].astype(bf16)
+    u_x = paired(u, "batch", 1)
+    d_y = paired(d, "batch", 2)
+    u_far = paired(jnp.stack([u, u_x]), "batch", 2)
+    d_far = paired(jnp.stack([d, d_y]), "batch", 1)
+    u_half = jnp.stack([u, u_x, u_far[0], u_far[1]])
+    d_half = jnp.stack([d, d_far[0], d_y, d_far[1]])
+    other = swap(jnp.stack([u_half, d_half]))
+    quarters = jnp.arange(nb, dtype=jnp.int32) ^ b
+    order = jnp.concatenate(
+        [jnp.where(f == 0, 0, nb) + quarters, jnp.where(f == 0, nb, 0) + quarters]
+    ).astype(jnp.int32)
+    return place(
+        order,
+        jnp.concatenate([u_half, other[0]], axis=0),
+        jnp.concatenate([d_half, other[1]], axis=0),
+    )
+
+
 def local(
     tokens,
     cotangent,
@@ -361,9 +491,6 @@
     width_local = w_qkv.shape[2]
     group = width_local // 2
     frame_slots = clip_of_frame.shape[1]
-    hidden_local = w_up.shape[1]
-    half = hidden_local // 2
-    quarter = half // nb
     blocks = length // BLOCK
 
     tokens_local = tokens[0, 0]
@@ -398,6 +525,14 @@
     tokens_all = lax.all_gather(tokens_local, "tensor", axis=0, tiled=True)
     mod_whole = lax.all_gather(mod_part, "tensor", axis=1, tiled=True)
 
+    all_unit = jnp.where(
+        all_bucket[:, 0] == 0, FRAME_SMALL // BLOCK, FRAME_LARGE // BLOCK
+    ).astype(jnp.int32)
+    all_frame = block_index[None, :] // all_unit[:, None]
+    picked = (all_frame[:, :, None] == frame_ids[None, None, :]).astype(f32)
+    cond_blocks = jnp.einsum("bif,bfd->bid", picked, cond_all.astype(f32), precision=highest)
+    mod_whole, cond_blocks = lax.optimization_barrier((mod_whole, cond_blocks))
+
     own_frames = lax.dynamic_slice(block_frame, (f * tz,), (tz,))
     local_frame = lax.dynamic_index_in_dim(own_frames, z, keepdims=False)
     mod_row = lax.dynamic_slice(mod_whole, (local_frame, 0), (1, 6 * width))
@@ -411,13 +546,10 @@
         [mine.reshape(width, 3 * group), theirs.reshape(width, 3 * group)], axis=1
     )
 
-    start = f * half + b * quarter
-    up_piece = lax.dynamic_slice(w_up.T, (start, 0), (quarter, width))
-    down_piece = lax.dynamic_slice(w_down, (start, 0), (quarter, width))
-    pieces = jnp.stack([up_piece, down_piece])
-    gathered = lax.all_gather(pieces, ("batch", "tensor"), axis=1, tiled=True)
-    up_t, down = gathered[0], gathered[1]
-    out_whole = lax.all_gather(w_out, "tensor", axis=0, tiled=True)
+    up_t, down = gather_hidden(w_up.T, w_down)
+    out_rows = w_out.shape[0] // (2 * nb)
+    out_piece = lax.dynamic_slice(w_out, ((f * nb + b) * out_rows, 0), (out_rows, width))
+    out_whole = lax.all_gather(out_piece, ("tensor", "frames", "batch"), axis=0, tiled=True)
 
     cos_all, sin_all = rotary_tables(jnp.arange(length, dtype=jnp.int32), group)
     cos_own = lax.dynamic_slice(cos_all, (f * shard_rows, 0), (shard_rows, group))
@@ -500,20 +632,17 @@
     frame_sums = jnp.concatenate(
         [sum_shift_one, sum_scale_one, own_slot[:, None] * local_sums[None, :]], axis=1
     )
-    share = lax.psum_scatter(frame_sums, "tensor", scatter_dimension=1, tiled=True)
+    share = jnp.sum(
+        lax.all_to_all(
+            frame_sums.reshape(tz, tz, -1).swapaxes(0, 1), "tensor", 0, 0, tiled=True
+        ),
+        axis=0,
+    )
     shares = lax.all_gather(share, ("batch", "frames"), axis=0, tiled=True)
-    all_unit = jnp.where(
-        all_bucket[:, 0] == 0, FRAME_SMALL // BLOCK, FRAME_LARGE // BLOCK
-    ).astype(jnp.int32)
-    all_frame = block_index[None, :] // all_unit[:, None]
-    picked = (all_frame[:, :, None] == frame_ids[None, None, :]).astype(f32)
-    cond_blocks = jnp.einsum("bif,bfd->bid", picked, cond_all.astype(f32), precision=highest)
     grad_w_mod = mm_highest(cond_blocks.reshape(nb * blocks, width), shares)
     grad_b_mod = jnp.sum(shares, axis=0)
 
-    grad_attn_in = lax.psum_scatter(
-        grad_attn_part.astype(bf16), "tensor", scatter_dimension=0, tiled=True
-    ).astype(f32)
+    grad_attn_in = collect_rows(grad_attn_part.astype(bf16), rows)
     grad_tokens = grad_mixed_one + norm_back(
         grad_attn_in * (1.0 + scale_one), normed_one, inverse_one
     )
@@ -529,17 +658,15 @@
         axis=2,
     ).reshape(width, 3, width_local)
     grad_w_qkv = lax.psum(grad_w_qkv.astype(bf16), ("frames", "batch")).astype(f32)
-    grad_w_out = lax.psum(
-        lax.psum_scatter(grad_out_weights, "tensor", scatter_dimension=0, tiled=True),
+    grad_w_out = lax.all_gather(
+        lax.psum_scatter(
+            grad_out_weights, ("tensor", "frames", "batch"), scatter_dimension=0, tiled=True
+        ),
         ("frames", "batch"),
+        axis=0,
+        tiled=True,
     ).astype(f32)
-
-    def reduce_rows(grad):
-        shard = lax.psum_scatter(grad, ("batch", "tensor"), scatter_dimension=0, tiled=True)
-        return lax.all_gather(shard, ("frames", "batch"), axis=0, tiled=True).astype(f32)
-
-    grad_w_down = reduce_rows(grad_down)
-    grad_w_up = reduce_rows(grad_up_t).T
+    grad_w_up, grad_w_down = reduce_hidden(grad_up_t, grad_down)
     return (
         result.reshape(1, 1, rows, width),
         grad_tokens.astype(bf16).reshape(1, 1, rows, width),

time: 755 us -> 681 us (0.902)
  waiting for transfers between devices: 479 us -> 215 us
  blocking collectives: 32.8 us -> 109 us
  starting transfers between devices: 20 us -> 82 us
  local copies, waits for them, and re-layouts: 38.1 us -> 94.3 us
  Pallas kernels: 66.1 us -> 39 us
  other arithmetic: 37.5 us -> 61.6 us
    all_gather x4 -> x1, waiting for transfers between devices: 151 us -> 0.02 us  [local(): lax.all_gather(out_piece, ('tensor', 'frames', 'batch'), axis=0, tiled=True)]
    reduce_scatter x4 -> x1, waiting for transfers between devices: 180 us -> 75 us  [local(): lax.psum_scatter(grad_out_weights, ('tensor', 'frames', 'batch'), scatter...]
    ppermute x0 -> x29, waiting for transfers between devices: none -> 95.3 us  [paired(): return lax.ppermute(value, axis, [(i, i ^ step) for i in range(count)])]
    ppermute x0 -> x29, starting transfers between devices: none -> 68.3 us  [paired(): return lax.ppermute(value, axis, [(i, i ^ step) for i in range(count)])]
    all_gather x1, blocking collectives: 16.8 us -> 68.7 us  [local(): mod_whole = lax.all_gather(mod_part, 'tensor', axis=1, tiled=True)]
    unnamed x12 -> x4, waiting for transfers between devices: 52.4 us -> 0.73 us
    psum x1, waiting for transfers between devices: 46.6 us -> 0.01 us  [local(): lax.psum(grad_w_qkv.astype(bf16), ('frames', 'batch')).astype(f32)]
    all_to_all x0 -> x1, waiting for transfers between devices: none -> 33.1 us  [local(): lax.all_to_all(frame_sums.reshape(tz, tz, -1).swapaxes(0, 1), 'tensor', 0...]
  transfers between devices with their start and end apart: 19 -> 43, of which waited for: 15 -> 18; matrix products, arithmetic and copies ran while one was open for 15% -> 30% of each run, Pallas kernels for 9% -> 6%
where the time goes in v2:
time: 681 us; the launch traced here: 669 us
  waiting for transfers between devices  215 us (32%)
  blocking collectives  109 us (16%)
  local copies, waits for them, and re-layouts  94.3 us (14%)
  starting transfers between devices  82 us (12%)
  other arithmetic  61.6 us (9%)
  matrix products  50.1 us (7%)
  Pallas kernels  39 us (6%)
  between operations  18.4 us (3%)
    ppermute x29, waiting for transfers between devices, paired(): return lax.ppermute(value, axis, [(i, i ^ step) for i in range(count)])  95.3 us
    reduce_scatter x1, waiting for transfers between devices, local(): lax.psum_scatter(grad_out_weights, ('tensor', 'frames', 'batch'), scatter...  75 us
    all_gather x1, blocking collectives, local(): mod_whole = lax.all_gather(mod_part, 'tensor', axis=1, tiled=True)  68.7 us
    ppermute x29, starting transfers between devices, paired(): return lax.ppermute(value, axis, [(i, i ^ step) for i in range(count)])  68.3 us
    unnamed x116, local copies, waits for them, and re-layouts  45.2 us
    dot_general x11, matrix products, mm(): lax.dot_general(left, right, (((contract_left,), (contract_right,)), ((),...  39.8 us
    all_to_all x1, waiting for transfers between devices, local(): lax.all_to_all(frame_sums.reshape(tz, tz, -1).swapaxes(0, 1), 'tensor', 0...  33.1 us
    all_gather x1, blocking collectives, local(): lax.all_gather(lax.psum_scatter(grad_out_weights, ('tensor', 'frames', 'b...  24.7 us
  transfers between devices with their start and end apart: 43, of which 18 were waited for; matrix products, arithmetic and copies ran while one was open for 30% of the time, Pallas kernels for 6%

profile of v2, /device:TPU:0, one launch (start us, length us, event | category | flops | bytes accessed | tf_op | source)
XLA Modules:
  0.0 669.5 jit_solution(11318790372823490545)
XLA Ops:
  14.0 3.1 collective-permute-start.2
  17.0 2.6 collective-permute-start.5
  23.8 7.6 %all-reduce = s32[36]{0:T(128)S(1)} all-reduce(s32[36]{0:T(128)S(1)} %add_dynamic-update-slice_fusion), channel_id=2, replica_groups=mesh['tensor'=4,'frames'=2,'batch'=4] {'batch'}, use_global_device_ids=true, to_apply=%add | all-reduce | flops 36 | bytes 288
  31.6 2.7 gather_fusion
  34.4 3.5 gather_fusion.1
  38.5 68.7 %all_gather.21 = f32[8,6144]{1,0:T(8,128)S(1)} all-gather(f32[8,1536]{1,0:T(8,128)S(1)} %convolution_add_fusion), channel_id=1, replica_groups=mesh['tensor'=4,'frames'=2,'batch'=4] {'tensor'}, dimensions={1}, use_global_device_ids=true | all-gather | bytes 245760 | tf_op jit(solution)/shard_map/all_gather | solution.py:526
  127.6 5.5 fusion.34
  133.1 5.1 pad_maximum_fusion.5
  142.2 2.7 constant_dynamic-slice_fusion.11
  161.9 3.7 collective-permute-done.3
  168.6 8.2 %collective-permute-done.7 = bf16[2,128,1024]{2,1,0:T(8,128)(2,1)S(1)} collective-permute-done((bf16[2,128,1024]{2,1,0:T(8,128)(2,1)S(1)}, bf16[2,128,1024]{2,1,0:T(8,128)(2,1)S(1)}, u32[]{:S(2)}, u32[]{:S(2)}) %collective-permute-start.7) | collective-permute-done | bytes 524320 | tf_op jit(solution)/shard_map/ppermute | solution.py:341
  179.2 9.0 %collective-permute-done.4 = bf16[2,1,128,1024]{3,2,1,0:T(8,128)(2,1)S(1)} collective-permute-done((bf16[2,1,128,1024]{3,2,1,0:T(8,128)(2,1)S(1)}, bf16[2,1,128,1024]{3,2,1,0:T(8,128)(2,1)S(1)}, u32[]{:S(2)}, u32[]{:S(2)}) %collective-permute-start.4) | collective-permute-done | bytes 524320 | tf_op jit(solution)/shard_map/ppermute | solution.py:341
  194.4 16.1 %collective-permute-done.8 = bf16[2,2,128,1024]{3,2,1,0:T(8,128)(2,1)S(1)} collective-permute-done((bf16[2,2,128,1024]{3,2,1,0:T(8,128)(2,1)S(1)}, bf16[2,2,128,1024]{3,2,1,0:T(8,128)(2,1)S(1)}, u32[]{:S(2)}, u32[]{:S(2)}) %collective-permute-start.8) | collective-permute-done | bytes 1048608 | tf_op jit(solution)/shard_map/ppermute | solution.py:341
  213.8 7.5 %project.1 = (bf16[1024,1024]{1,0:T(8,128)(2,1)}, bf16[2,3,1024,128]{3,2,1,0:T(8,128)(2,1)}) custom-call(s32[4]{0:T(128)} %dynamic_slice.67.frame_ref, bf16[1024,1024]{1,0:T(8,128)(2,1)} %bitcast.301, f32[8,2048]{1,0:T(8,128)} %slice.271.mod_ref, bf16[1024,768]{1,0:T(8,128)(2,1)} %pad_maximum_fusion.2.w_ref, ...), custom_call_target="tpu_custom_call" | custom-call | tf_op jit(solution)/shard_map/project/pallas_call | solution.py:88
  228.2 9.8 %attend.1 = (bf16[8,128,256]{2,1,0:T(8,128)(2,1)}, f32[8,8,256]{2,1,0:T(8,128)}) custom-call(s32[8]{0:T(128)} %select_reduce_fusion.lo_ref, s32[8]{0:T(128)} %add_multiply_fusion.1.hi_ref, s32[1]{0:T(128)S(6)} %copy.186.flag_ref, bf16[3,2048,128]{2,1,0:T(8,128)(2,1)} %pad_maximum_fusion.3.q_ref.k_ref.v_ref, ...), custom_call_target="tpu_custom_call" | custom-call | tf_op jit(solution)/shard_map/attend/pallas_call | solution.py:185
  238.0 4.8 all-to-all-start
  248.1 9.5 %all-to-all-done = bf16[8,128,256]{2,1,0:T(8,128)(2,1)S(1)} async-done(((bf16[8,128,256]{2,1,0:T(8,128)(2,1)}), bf16[8,128,256]{2,1,0:T(8,128)(2,1)S(1)}, u32[]{:S(2)}, u32[]{:S(2)}) %all-to-all-start) | async-done | bytes 524320 | tf_op jit(solution)/shard_map/all_to_all | solution.py:569
  258.5 2.8 fusion.84
  263.8 4.6 fusion.31
  268.3 4.9 fusion.82
  273.5 7.0 %fusion.9 = bf16[512,2048]{1,0:T(8,128)(2,1)S(1)} fusion(f32[512,2048]{1,0:T(8,128)S(1)} %fusion.31, bf16[2048,1024]{1,0:T(8,128)(2,1)} %fusion.41, bf16[256,1024]{1,0:T(8,128)(2,1)} %collective-permute-done.14, bf16[256,1024]{1,0:T(8,128)(2,1)} %fusion.23), kind=kOutput, calls=%fused_computation.15 | convolution fusion | flops 2170552320 | bytes 11534336 | tf_op jit(solution)/shard_map/dot_general | solution.py:327
  280.6 4.7 fusion.97
  285.9 4.2 convolution_convert_fusion
  292.8 17.6 %collective-permute-start.22 = (bf16[2,2,128,1024]{3,2,0,1:T(8,128)(2,1)}, bf16[2,2,128,1024]{3,2,0,1:T(8,128)(2,1)}, u32[]{:S(2)}, u32[]{:S(2)}) collective-permute-start(bf16[2,2,128,1024]{3,2,0,1:T(8,128)(2,1)} %pad_maximum_fusion.11), channel_id=1, source_target_pairs={{0,1},{1,0},{2,3},{3,2},{4,5},{5,4},{6,7},{7,6},{8,9},{9,8},{10,11... | collective-permute-start | bytes 3145736 | tf_op jit(solution)/shard_map/ppermute | solution.py:341
  327.2 4.2 all-to-all-start.1
  331.6 3.1 collective-permute-done.22
  339.2 2.6 collective-permute-done.20
  344.0 13.1 %collective-permute-done.26 = bf16[2,2,128,1024]{3,2,0,1:T(8,128)(2,1)} collective-permute-done((bf16[2,2,128,1024]{3,2,0,1:T(8,128)(2,1)}, bf16[2,2,128,1024]{3,2,0,1:T(8,128)(2,1)}, u32[]{:S(2)}, u32[]{:S(2)}) %collective-permute-start.26) | collective-permute-done | bytes 1048608 | tf_op jit(solution)/shard_map/ppermute | solution.py:341
  361.3 3.0 collective-permute-done.24
  366.5 8.9 %collective-permute-done.23 = bf16[2,128,1024]{2,1,0:T(8,128)(2,1)S(1)} collective-permute-done((bf16[2,128,1024]{2,1,0:T(8,128)(2,1)S(1)}, bf16[2,128,1024]{2,1,0:T(8,128)(2,1)S(1)}, u32[]{:S(2)}, u32[]{:S(2)}) %collective-permute-start.23) | collective-permute-done | bytes 524320 | tf_op jit(solution)/shard_map/ppermute | solution.py:341
  377.5 8.1 %collective-permute-done.27 = bf16[2,128,1024]{2,1,0:T(8,128)(2,1)S(1)} collective-permute-done((bf16[2,128,1024]{2,1,0:T(8,128)(2,1)S(1)}, bf16[2,128,1024]{2,1,0:T(8,128)(2,1)S(1)}, u32[]{:S(2)}, u32[]{:S(2)}) %collective-permute-start.27) | collective-permute-done | bytes 524320 | tf_op jit(solution)/shard_map/ppermute | solution.py:341
  388.9 13.6 %attend_back.1 = bf16[3,2048,128]{2,1,0:T(8,128)(2,1)} custom-call(s32[8]{0:T(128)} %select_reduce_fusion.lo_ref, s32[8]{0:T(128)} %add_multiply_fusion.1.hi_ref, s32[1]{0:T(128)S(6)} %copy.186.flag_ref, bf16[3,2048,128]{2,1,0:T(8,128)(2,1)} %pad_maximum_fusion.3.q_ref.k_ref.v_ref, bf16[3,2048,128]{2,1,0:T(8,128)(2,1)} %pad_maximum_fusion.3.q_ref.k_ref.v_ref, ...), custom_call_target="tpu_custom_call" | custom-call | tf_op jit(solution)/shard_map/attend_back/pallas_call | solution.py:299
  410.0 4.9 copy.114
  414.9 3.8 convert_element_type.242
  419.1 13.7 %collective-permute-done.28 = bf16[2,128,1024]{2,1,0:T(8,128)(2,1)} collective-permute-done((bf16[2,128,1024]{2,1,0:T(8,128)(2,1)}, bf16[2,128,1024]{2,1,0:T(8,128)(2,1)}, u32[]{:S(2)}, u32[]{:S(2)}) %collective-permute-start.28) | collective-permute-done | bytes 524320 | tf_op jit(solution)/shard_map/ppermute | solution.py:341
  435.5 19.4 %collective-permute-start.33 = (bf16[128,1024]{1,0:T(8,128)(2,1)}, bf16[128,1024]{1,0:T(8,128)(2,1)}, u32[]{:S(2)}, u32[]{:S(2)}) collective-permute-start(bf16[128,1024]{1,0:T(8,128)(2,1)} %bitcast.94), channel_id=1, source_target_pairs={{0,2},{1,3},{2,0},{3,1},{4,6},{5,7},{6,4},{7,5},{8,10},{9,11},{10,... | collective-permute-start | bytes 786440 | tf_op jit(solution)/shard_map/ppermute | solution.py:341
  457.9 5.3 collective-permute-done.33
  468.1 3.7 fusion.96
  474.7 4.0 collective-permute-start.17
  487.7 3.3 all-to-all-start.2
  491.0 33.1 %all-to-all-done.2 = f32[4,4,1536]{2,1,0:T(4,128)S(1)} async-done(((f32[4,4,1536]{2,1,0:T(4,128)}), f32[4,4,1536]{2,1,0:T(4,128)S(1)}, u32[]{:S(2)}, u32[]{:S(2)}) %all-to-all-start.2) | async-done | bytes 98336 | tf_op jit(solution)/shard_map/all_to_all | solution.py:636
  524.2 7.8 %all-gather.2 = f32[8,4,1536]{2,1,0:T(4,128)S(1)} all-gather(f32[1,4,1536]{2,1,0:T(4,128)S(1)} %bitcast.320), channel_id=1, replica_groups=mesh['tensor'=4,'frames'=2,'batch'=4] {'batch','frames'}, dimensions={0}, use_global_device_ids=true | all-gather | bytes 221184 | tf_op jit(solution)/shard_map/all_gather | solution.py:641
  532.7 7.9 %fusion.57 = f32[1024,1536]{1,0:T(8,128)} fusion(f32[32,1536]{1,0:T(8,128)S(1)} %reshape.408, f32[4,8,1024]{2,1,0:T(8,128)} %fusion.59), kind=kOutput, calls=%fused_computation.190 | convolution fusion | flops 603979776 | bytes 6619136 | tf_op jit(solution)/shard_map/dot_general | solution.py:683
  544.0 3.4 convert_element_type.243
  548.7 2.5 pad_maximum_fusion.1.up_ref
  553.6 8.1 %place.1 = (f32[1024,1024]{1,0:T(8,128)}, f32[1024,1024]{1,0:T(8,128)}) custom-call(s32[8]{0:T(128)} %pad_add_fusion.order_ref, bf16[8,128,1024]{2,1,0:T(8,128)(2,1)} %pad_maximum_fusion.1.up_ref, bf16[8,128,1024]{2,1,0:T(8,128)(2,1)} %fusion.25.down_ref), custom_call_target="tpu_custom_call" | custom-call | tf_op jit(solution)/shard_map/place/pallas_call | solution.py:402
  561.7 75.0 %reduce-scatter.2.cloned.1.call-done = bf16[32,1024]{1,0:T(8,128)(2,1)} async-done(((bf16[1024,1024]{1,0:T(8,128)(2,1)}), bf16[32,1024]{1,0:T(8,128)(2,1)}) %reduce-scatter.2.cloned.1.call-update) | async-done | bytes 65552 | tf_op jit(solution)/shard_map/reduce_scatter | solution.py:662
  636.7 24.7 %all_gather.27 = bf16[256,1024]{1,0:T(8,128)(2,1)S(1)} all-gather(bf16[32,1024]{1,0:T(8,128)(2,1)} %reduce-scatter.2.cloned.1.call-done), channel_id=1, replica_groups=mesh['tensor'=4,'frames'=2,'batch'=4] {'frames','batch'}, dimensions={0}, use_global_device_ids=true | all-gather | bytes 589824 | tf_op jit(solution)/shard_map/all_gather | solution.py:661
  (306 shorter events, 158.0 us)
Async XLA Ops:
  7.2 206.6 %all-gather.8.cloned.1.call-start = ((), (), s32[]{:S(2)}) async-start(), calls=%async_computation.7 | async-start | bytes 2621440 | tf_op jit(solution)/shard_map/all_gather | solution.py:525
  8.0 240.2 %all-gather.6.cloned.1.call-start = ((), (), s32[]{:S(2)}) async-start(), calls=%async_computation.4 | async-start | bytes 2162688 | tf_op jit(solution)/shard_map/all_gather | solution.py:552
  14.0 138.3 %collective-permute-start.2 = (bf16[2,128,1024]{2,1,0:T(8,128)(2,1)}, bf16[2,128,1024]{2,1,0:T(8,128)(2,1)}, u32[]{:S(2)}, u32[]{:S(2)}) collective-permute-start(bf16[2,128,1024]{2,1,0:T(8,128)(2,1)} %pad_maximum_fusion.19), channel_id=1, source_target_pairs={{0,8},{8,0},{16,24},{24,16},{1,9},{9,1},{17,25},{25,17},{2,10},{10... | collective-permute-start | bytes 1572872 | tf_op jit(solution)/shard_map/ppermute | solution.py:341
  17.0 140.6 %collective-permute-start.5 = (bf16[2,128,1024]{2,1,0:T(8,128)(2,1)}, bf16[2,128,1024]{2,1,0:T(8,128)(2,1)}, u32[]{:S(2)}, u32[]{:S(2)}) collective-permute-start(bf16[2,128,1024]{2,1,0:T(8,128)(2,1)} %pad_maximum_fusion.19), channel_id=1, source_target_pairs={{0,16},{8,24},{16,0},{24,8},{1,17},{9,25},{17,1},{25,9},{2,18},{10... | collective-permute-start | bytes 1572872 | tf_op jit(solution)/shard_map/ppermute | solution.py:341
  19.6 136.9 %collective-permute-start.6 = (bf16[2,128,1024]{2,1,0:T(8,128)(2,1)}, bf16[2,128,1024]{2,1,0:T(8,128)(2,1)}, u32[]{:S(2)}, u32[]{:S(2)}) collective-permute-start(bf16[2,128,1024]{2,1,0:T(8,128)(2,1)} %pad_maximum_fusion.19), channel_id=1, source_target_pairs={{0,24},{8,16},{16,8},{24,0},{1,25},{9,17},{17,9},{25,1},{2,26},{10... | collective-permute-start | bytes 1572872 | tf_op jit(solution)/shard_map/ppermute | solution.py:341
  37.9 87.1 %copy-start.33 = (s32[1,8]{1,0:T(1,128)S(1)}, s32[1,8]{1,0:T(1,128)}, u32[]{:S(2)}) copy-start(s32[1,8]{1,0:T(1,128)} %param.15) | copy-start | bytes 100
  38.5 80.6 %copy-start.23 = (bf16[1024,128]{1,0:T(8,128)(2,1)S(1)}, bf16[1024,128]{1,0:T(8,128)(2,1)}, u32[]{:S(2)}) copy-start(bf16[1024,128]{1,0:T(8,128)(2,1)} %get-tuple-element.65) | copy-start | bytes 786436
  38.5 87.4 %copy-start.21 = (bf16[1024,3,256]{2,0,1:T(8,128)(2,1)S(1)}, bf16[1024,3,256]{2,0,1:T(8,128)(2,1)}, u32[]{:S(2)}) copy-start(bf16[1024,3,256]{2,0,1:T(8,128)(2,1)} %param.20) | copy-start | bytes 4718596
  112.1 161.4 %collective-permute-start.14 = (bf16[256,1024]{1,0:T(8,128)(2,1)}, bf16[256,1024]{1,0:T(8,128)(2,1)}, u32[]{:S(2)}, u32[]{:S(2)}) collective-permute-start(bf16[256,1024]{1,0:T(8,128)(2,1)} %fusion.23), channel_id=1, source_target_pairs={{0,4},{4,0},{1,5},{5,1},{2,6},{6,2},{3,7},{7,3},{8,12},{12,8},{9,1... | collective-permute-start | bytes 1572872 | tf_op jit(solution)/shard_map/ppermute | solution.py:336
  153.5 12.1 %collective-permute-start.3 = (bf16[1,128,1024]{2,1,0:T(8,128)(2,1)S(1)}, bf16[1,128,1024]{2,1,0:T(8,128)(2,1)S(1)}, u32[]{:S(2)}, u32[]{:S(2)}) collective-permute-start(bf16[1,128,1024]{2,1,0:T(8,128)(2,1)S(1)} %get-tuple-element.105), channel_id=1, source_target_pairs={{0,1},{1,0},{2,3},{3,2},{4,5},{5,4},{6,7},{7,6},{8,9},{9,8},{10,11... | collective-permute-start | bytes 786440 | tf_op jit(solution)/shard_map/ppermute | solution.py:341
  155.0 12.2 %collective-permute-start.9 = (bf16[1,128,1024]{2,1,0:T(8,128)(2,1)S(1)}, bf16[1,128,1024]{2,1,0:T(8,128)(2,1)S(1)}, u32[]{:S(2)}, u32[]{:S(2)}) collective-permute-start(bf16[1,128,1024]{2,1,0:T(8,128)(2,1)S(1)} %get-tuple-element.104), channel_id=1, source_target_pairs={{0,2},{1,3},{2,0},{3,1},{4,6},{5,7},{6,4},{7,5},{8,10},{9,11},{10,... | collective-permute-start | bytes 786440 | tf_op jit(solution)/shard_map/ppermute | solution.py:341
  158.8 18.0 %collective-permute-start.7 = (bf16[2,128,1024]{2,1,0:T(8,128)(2,1)S(1)}, bf16[2,128,1024]{2,1,0:T(8,128)(2,1)S(1)}, u32[]{:S(2)}, u32[]{:S(2)}) collective-permute-start(bf16[2,128,1024]{2,1,0:T(8,128)(2,1)S(1)} %get-tuple-element.95), channel_id=1, source_target_pairs={{0,1},{1,0},{2,3},{3,2},{4,5},{5,4},{6,7},{7,6},{8,9},{9,8},{10,11... | collective-permute-start | bytes 1572872 | tf_op jit(solution)/shard_map/ppermute | solution.py:341
  159.5 19.0 %collective-permute-start.11 = (bf16[2,128,1024]{2,1,0:T(8,128)(2,1)S(1)}, bf16[2,128,1024]{2,1,0:T(8,128)(2,1)S(1)}, u32[]{:S(2)}, u32[]{:S(2)}) collective-permute-start(bf16[2,128,1024]{2,1,0:T(8,128)(2,1)S(1)} %get-tuple-element.109), channel_id=1, source_target_pairs={{0,2},{1,3},{2,0},{3,1},{4,6},{5,7},{6,4},{7,5},{8,10},{9,11},{10,... | collective-permute-start | bytes 1572872 | tf_op jit(solution)/shard_map/ppermute | solution.py:341
  165.6 22.6 %collective-permute-start.4 = (bf16[2,1,128,1024]{3,2,1,0:T(8,128)(2,1)S(1)}, bf16[2,1,128,1024]{3,2,1,0:T(8,128)(2,1)S(1)}, u32[]{:S(2)}, u32[]{:S(2)}) collective-permute-start(bf16[2,1,128,1024]{3,2,1,0:T(8,128)(2,1)S(1)} %pad_maximum_fusion.20), channel_id=1, source_target_pairs={{0,2},{1,3},{2,0},{3,1},{4,6},{5,7},{6,4},{7,5},{8,10},{9,11},{10,... | collective-permute-start | bytes 1572872 | tf_op jit(solution)/shard_map/ppermute | solution.py:341
  167.2 22.4 %collective-permute-start.10 = (bf16[2,1,128,1024]{3,2,1,0:T(8,128)(2,1)S(1)}, bf16[2,1,128,1024]{3,2,1,0:T(8,128)(2,1)S(1)}, u32[]{:S(2)}, u32[]{:S(2)}) collective-permute-start(bf16[2,1,128,1024]{3,2,1,0:T(8,128)(2,1)S(1)} %pad_maximum_fusion.22), channel_id=1, source_target_pairs={{0,1},{1,0},{2,3},{3,2},{4,5},{5,4},{6,7},{7,6},{8,9},{9,8},{10,11... | collective-permute-start | bytes 1572872 | tf_op jit(solution)/shard_map/ppermute | solution.py:341
  176.9 33.5 %collective-permute-start.8 = (bf16[2,2,128,1024]{3,2,1,0:T(8,128)(2,1)S(1)}, bf16[2,2,128,1024]{3,2,1,0:T(8,128)(2,1)S(1)}, u32[]{:S(2)}, u32[]{:S(2)}) collective-permute-start(bf16[2,2,128,1024]{3,2,1,0:T(8,128)(2,1)S(1)} %pad_maximum_fusion.8), channel_id=1, source_target_pairs={{0,2},{1,3},{2,0},{3,1},{4,6},{5,7},{6,4},{7,5},{8,10},{9,11},{10,... | collective-permute-start | bytes 3145736 | tf_op jit(solution)/shard_map/ppermute | solution.py:341
  178.6 33.7 %collective-permute-start.12 = (bf16[2,2,128,1024]{3,2,1,0:T(8,128)(2,1)S(1)}, bf16[2,2,128,1024]{3,2,1,0:T(8,128)(2,1)S(1)}, u32[]{:S(2)}, u32[]{:S(2)}) collective-permute-start(bf16[2,2,128,1024]{3,2,1,0:T(8,128)(2,1)S(1)} %pad_maximum_fusion.9), channel_id=1, source_target_pairs={{0,1},{1,0},{2,3},{3,2},{4,5},{5,4},{6,7},{7,6},{8,9},{9,8},{10,11... | collective-permute-start | bytes 3145736 | tf_op jit(solution)/shard_map/ppermute | solution.py:341
  222.6 4.2 collective-permute-start
  238.0 19.6 %all-to-all-start = ((bf16[8,128,256]{2,1,0:T(8,128)(2,1)}), bf16[8,128,256]{2,1,0:T(8,128)(2,1)S(1)}, u32[]{:S(2)}, u32[]{:S(2)}) async-start(bf16[8,128,256]{2,1,0:T(8,128)(2,1)} %get-tuple-element.18.o_ref), calls=%async_computation | async-start | bytes 1048576 | tf_op jit(solution)/shard_map/all_to_all | solution.py:569
  261.8 2.0 collective-permute-start.1
  273.3 49.8 %collective-permute-start.13 = (f32[256,1024]{1,0:T(8,128)S(1)}, f32[256,1024]{1,0:T(8,128)S(1)}, u32[]{:S(2)}, u32[]{:S(2)}) collective-permute-start(f32[256,1024]{1,0:T(8,128)S(1)} %slice.383), channel_id=1, source_target_pairs={{0,4},{4,0},{1,5},{5,1},{2,6},{6,2},{3,7},{7,3},{8,12},{12,8},{9,1... | collective-permute-start | bytes 3145736 | tf_op jit(solution)/shard_map/ppermute | solution.py:336
  285.4 37.1 %collective-permute-start.15 = (f32[256,1024]{1,0:T(8,128)S(1)}, f32[256,1024]{1,0:T(8,128)S(1)}, u32[]{:S(2)}, u32[]{:S(2)}) collective-permute-start(f32[256,1024]{1,0:T(8,128)S(1)} %slice.385), channel_id=1, source_target_pairs={{0,4},{4,0},{1,5},{5,1},{2,6},{6,2},{3,7},{7,3},{8,12},{12,8},{9,1... | collective-permute-start | bytes 3145736 | tf_op jit(solution)/shard_map/ppermute | solution.py:336
  292.8 41.9 %collective-permute-start.22 = (bf16[2,2,128,1024]{3,2,0,1:T(8,128)(2,1)}, bf16[2,2,128,1024]{3,2,0,1:T(8,128)(2,1)}, u32[]{:S(2)}, u32[]{:S(2)}) collective-permute-start(bf16[2,2,128,1024]{3,2,0,1:T(8,128)(2,1)} %pad_maximum_fusion.11), channel_id=1, source_target_pairs={{0,1},{1,0},{2,3},{3,2},{4,5},{5,4},{6,7},{7,6},{8,9},{9,8},{10,11... | collective-permute-start | bytes 3145736 | tf_op jit(solution)/shard_map/ppermute | solution.py:341
  315.5 26.3 %collective-permute-start.20 = (bf16[2,2,128,1024]{3,2,0,1:T(8,128)(2,1)}, bf16[2,2,128,1024]{3,2,0,1:T(8,128)(2,1)}, u32[]{:S(2)}, u32[]{:S(2)}) collective-permute-start(bf16[2,2,128,1024]{3,2,0,1:T(8,128)(2,1)} %copy.132), channel_id=1, source_target_pairs={{0,2},{1,3},{2,0},{3,1},{4,6},{5,7},{6,4},{7,5},{8,10},{9,11},{10,... | collective-permute-start | bytes 3145736 | tf_op jit(solution)/shard_map/ppermute | solution.py:341
  319.3 37.9 %collective-permute-start.26 = (bf16[2,2,128,1024]{3,2,0,1:T(8,128)(2,1)}, bf16[2,2,128,1024]{3,2,0,1:T(8,128)(2,1)}, u32[]{:S(2)}, u32[]{:S(2)}) collective-permute-start(bf16[2,2,128,1024]{3,2,0,1:T(8,128)(2,1)} %pad_maximum_fusion.12), channel_id=1, source_target_pairs={{0,1},{1,0},{2,3},{3,2},{4,5},{5,4},{6,7},{7,6},{8,9},{9,8},{10,11... | collective-permute-start | bytes 3145736 | tf_op jit(solution)/shard_map/ppermute | solution.py:341
  322.5 41.8 %collective-permute-start.24 = (bf16[2,2,128,1024]{3,2,0,1:T(8,128)(2,1)}, bf16[2,2,128,1024]{3,2,0,1:T(8,128)(2,1)}, u32[]{:S(2)}, u32[]{:S(2)}) collective-permute-start(bf16[2,2,128,1024]{3,2,0,1:T(8,128)(2,1)} %copy.138), channel_id=1, source_target_pairs={{0,2},{1,3},{2,0},{3,1},{4,6},{5,7},{6,4},{7,5},{8,10},{9,11},{10,... | collective-permute-start | bytes 3145736 | tf_op jit(solution)/shard_map/ppermute | solution.py:341
  327.2 61.7 %all-to-all-start.1 = ((bf16[8,128,256]{2,1,0:T(8,128)(2,1)}), bf16[8,128,256]{2,1,0:T(8,128)(2,1)}, u32[]{:S(2)}, u32[]{:S(2)}) async-start(bf16[8,128,256]{2,1,0:T(8,128)(2,1)} %bitcast.319), calls=%async_computation.1 | async-start | bytes 1048576 | tf_op jit(solution)/shard_map/all_to_all | solution.py:603
  331.4 212.6 %all-reduce.3.cloned.1.call-start = ((), (), s32[]{:S(2)}) async-start(), calls=%async_computation.5 | async-start | bytes 3145728 | tf_op jit(solution)/shard_map/psum | solution.py:660
  336.7 38.7 %collective-permute-start.23 = (bf16[2,128,1024]{2,1,0:T(8,128)(2,1)S(1)}, bf16[2,128,1024]{2,1,0:T(8,128)(2,1)S(1)}, u32[]{:S(2)}, u32[]{:S(2)}) collective-permute-start(bf16[2,128,1024]{2,1,0:T(8,128)(2,1)S(1)} %slice_bitcast_fusion.11), channel_id=1, source_target_pairs={{0,2},{1,3},{2,0},{3,1},{4,6},{5,7},{6,4},{7,5},{8,10},{9,11},{10,... | collective-permute-start | bytes 1572872 | tf_op jit(solution)/shard_map/ppermute | solution.py:341
  343.6 32.0 %collective-permute-start.21 = (bf16[2,128,1024]{2,1,0:T(8,128)(2,1)S(1)}, bf16[2,128,1024]{2,1,0:T(8,128)(2,1)S(1)}, u32[]{:S(2)}, u32[]{:S(2)}) collective-permute-start(bf16[2,128,1024]{2,1,0:T(8,128)(2,1)S(1)} %slice_bitcast_fusion.17), channel_id=1, source_target_pairs={{0,1},{1,0},{2,3},{3,2},{4,5},{5,4},{6,7},{7,6},{8,9},{9,8},{10,11... | collective-permute-start | bytes 1572872 | tf_op jit(solution)/shard_map/ppermute | solution.py:341
  358.8 26.7 %collective-permute-start.27 = (bf16[2,128,1024]{2,1,0:T(8,128)(2,1)S(1)}, bf16[2,128,1024]{2,1,0:T(8,128)(2,1)S(1)}, u32[]{:S(2)}, u32[]{:S(2)}) collective-permute-start(bf16[2,128,1024]{2,1,0:T(8,128)(2,1)S(1)} %slice_bitcast_fusion.3), channel_id=1, source_target_pairs={{0,2},{1,3},{2,0},{3,1},{4,6},{5,7},{6,4},{7,5},{8,10},{9,11},{10,... | collective-permute-start | bytes 1572872 | tf_op jit(solution)/shard_map/ppermute | solution.py:341
  366.0 19.8 %collective-permute-start.25 = (bf16[2,128,1024]{2,1,0:T(8,128)(2,1)S(1)}, bf16[2,128,1024]{2,1,0:T(8,128)(2,1)S(1)}, u32[]{:S(2)}, u32[]{:S(2)}) collective-permute-start(bf16[2,128,1024]{2,1,0:T(8,128)(2,1)S(1)} %slice_bitcast_fusion.9), channel_id=1, source_target_pairs={{0,1},{1,0},{2,3},{3,2},{4,5},{5,4},{6,7},{7,6},{8,9},{9,8},{10,11... | collective-permute-start | bytes 1572872 | tf_op jit(solution)/shard_map/ppermute | solution.py:341
  377.5 41.6 %collective-permute-start.30 = (bf16[2,128,1024]{2,1,0:T(8,128)(2,1)}, bf16[2,128,1024]{2,1,0:T(8,128)(2,1)}, u32[]{:S(2)}, u32[]{:S(2)}) collective-permute-start(bf16[2,128,1024]{2,1,0:T(8,128)(2,1)} %pad_maximum_fusion.26), channel_id=1, source_target_pairs={{0,8},{8,0},{16,24},{24,16},{1,9},{9,1},{17,25},{25,17},{2,10},{10... | collective-permute-start | bytes 1572872 | tf_op jit(solution)/shard_map/ppermute | solution.py:341
  387.6 31.5 %collective-permute-start.29 = (bf16[2,128,1024]{2,1,0:T(8,128)(2,1)}, bf16[2,128,1024]{2,1,0:T(8,128)(2,1)}, u32[]{:S(2)}, u32[]{:S(2)}) collective-permute-start(bf16[2,128,1024]{2,1,0:T(8,128)(2,1)} %pad_maximum_fusion.25), channel_id=1, source_target_pairs={{0,24},{8,16},{16,8},{24,0},{1,25},{9,17},{17,9},{25,1},{2,26},{10... | collective-permute-start | bytes 1572872 | tf_op jit(solution)/shard_map/ppermute | solution.py:341
  404.1 2.4 collective-permute-start.16
  406.0 26.8 %collective-permute-start.28 = (bf16[2,128,1024]{2,1,0:T(8,128)(2,1)}, bf16[2,128,1024]{2,1,0:T(8,128)(2,1)}, u32[]{:S(2)}, u32[]{:S(2)}) collective-permute-start(bf16[2,128,1024]{2,1,0:T(8,128)(2,1)} %pad_maximum_fusion.24), channel_id=1, source_target_pairs={{0,16},{8,24},{16,0},{24,8},{1,17},{9,25},{17,1},{25,9},{2,18},{10... | collective-permute-start | bytes 1572872 | tf_op jit(solution)/shard_map/ppermute | solution.py:341
  418.8 217.9 %reduce-scatter.2.cloned.1.call-start = ((), (), s32[]{:S(2)}) async-start(), calls=%async_computation.6 | async-start | bytes 2162688 | tf_op jit(solution)/shard_map/reduce_scatter | solution.py:662
  435.5 27.6 %collective-permute-start.33 = (bf16[128,1024]{1,0:T(8,128)(2,1)}, bf16[128,1024]{1,0:T(8,128)(2,1)}, u32[]{:S(2)}, u32[]{:S(2)}) collective-permute-start(bf16[128,1024]{1,0:T(8,128)(2,1)} %bitcast.94), channel_id=1, source_target_pairs={{0,2},{1,3},{2,0},{3,1},{4,6},{5,7},{6,4},{7,5},{8,10},{9,11},{10,... | collective-permute-start | bytes 786440 | tf_op jit(solution)/shard_map/ppermute | solution.py:341
  454.8 10.3 %collective-permute-start.31 = (bf16[128,1024]{1,0:T(8,128)(2,1)S(1)}, bf16[128,1024]{1,0:T(8,128)(2,1)}, u32[]{:S(2)}, u32[]{:S(2)}) collective-permute-start(bf16[128,1024]{1,0:T(8,128)(2,1)S(1)} %bitcast.309), channel_id=1, source_target_pairs={{0,1},{1,0},{2,3},{3,2},{4,5},{5,4},{6,7},{7,6},{8,9},{9,8},{10,11... | collective-permute-start | bytes 786440 | tf_op jit(solution)/shard_map/ppermute | solution.py:341
  464.2 15.7 %collective-permute-start.34 = (bf16[2,128,1024]{2,1,0:T(8,128)(2,1)S(1)}, bf16[2,128,1024]{2,1,0:T(8,128)(2,1)S(1)}, u32[]{:S(2)}, u32[]{:S(2)}) collective-permute-start(bf16[2,128,1024]{2,1,0:T(8,128)(2,1)S(1)} %pad_maximum_fusion.28), channel_id=1, source_target_pairs={{0,1},{1,0},{2,3},{3,2},{4,5},{5,4},{6,7},{7,6},{8,9},{9,8},{10,11... | collective-permute-start | bytes 1572872 | tf_op jit(solution)/shard_map/ppermute | solution.py:341
  466.1 18.2 %collective-permute-start.32 = (bf16[2,128,1024]{2,1,0:T(8,128)(2,1)S(1)}, bf16[2,128,1024]{2,1,0:T(8,128)(2,1)S(1)}, u32[]{:S(2)}, u32[]{:S(2)}) collective-permute-start(bf16[2,128,1024]{2,1,0:T(8,128)(2,1)S(1)} %pad_maximum_fusion.27), channel_id=1, source_target_pairs={{0,2},{1,3},{2,0},{3,1},{4,6},{5,7},{6,4},{7,5},{8,10},{9,11},{10,... | collective-permute-start | bytes 1572872 | tf_op jit(solution)/shard_map/ppermute | solution.py:341
  474.3 66.4 %collective-permute-start.19 = (bf16[256,1024]{1,0:T(8,128)(2,1)}, bf16[256,1024]{1,0:T(8,128)(2,1)}, u32[]{:S(2)}, u32[]{:S(2)}) collective-permute-start(bf16[256,1024]{1,0:T(8,128)(2,1)} %get-tuple-element.63), channel_id=1, source_target_pairs={{0,8},{8,0},{16,24},{24,16},{1,9},{9,1},{17,25},{25,17},{2,10},{10... | collective-permute-start | bytes 1572872 | tf_op jit(solution)/shard_map/ppermute | solution.py:341
  474.3 66.4 %collective-permute-start.18 = (bf16[256,1024]{1,0:T(8,128)(2,1)}, bf16[256,1024]{1,0:T(8,128)(2,1)}, u32[]{:S(2)}, u32[]{:S(2)}) collective-permute-start(bf16[256,1024]{1,0:T(8,128)(2,1)} %get-tuple-element.64), channel_id=1, source_target_pairs={{0,16},{8,24},{16,0},{24,8},{1,17},{9,25},{17,1},{25,9},{2,18},{10... | collective-permute-start | bytes 1572872 | tf_op jit(solution)/shard_map/ppermute | solution.py:341
  474.7 66.0 %collective-permute-start.17 = (bf16[256,1024]{1,0:T(8,128)(2,1)}, bf16[256,1024]{1,0:T(8,128)(2,1)}, u32[]{:S(2)}, u32[]{:S(2)}) collective-permute-start(bf16[256,1024]{1,0:T(8,128)(2,1)} %get-tuple-element.62), channel_id=1, source_target_pairs={{0,24},{8,16},{16,8},{24,0},{1,25},{9,17},{17,9},{25,1},{2,26},{10... | collective-permute-start | bytes 1572872 | tf_op jit(solution)/shard_map/ppermute | solution.py:341
  487.1 53.6 %copy-start.3 = (bf16[1,1,256,1024]{3,2,1,0:T(8,128)(2,1)S(1)}, bf16[1,1,256,1024]{3,2,1,0:T(8,128)(2,1)}, u32[]{:S(2)}) copy-start(bf16[1,1,256,1024]{3,2,1,0:T(8,128)(2,1)} %param.12) | copy-start | bytes 1572868
  487.1 60.3 %collective-permute-start.35 = (bf16[2,4,128,1024]{3,2,1,0:T(8,128)(2,1)}, bf16[2,4,128,1024]{3,2,1,0:T(8,128)(2,1)}, u32[]{:S(2)}, u32[]{:S(2)}) collective-permute-start(bf16[2,4,128,1024]{3,2,1,0:T(8,128)(2,1)} %pad_maximum_fusion), channel_id=1, source_target_pairs={{0,4},{4,0},{1,5},{5,1},{2,6},{6,2},{3,7},{7,3},{8,12},{12,8},{9,1... | collective-permute-start | bytes 6291464 | tf_op jit(solution)/shard_map/ppermute | solution.py:336
  487.7 36.4 %all-to-all-start.2 = ((f32[4,4,1536]{2,1,0:T(4,128)}), f32[4,4,1536]{2,1,0:T(4,128)S(1)}, u32[]{:S(2)}, u32[]{:S(2)}) async-start(f32[4,4,1536]{2,1,0:T(4,128)} %bitcast.75), calls=%async_computation.2 | async-start | bytes 196608 | tf_op jit(solution)/shard_map/all_to_all | solution.py:636
  551.2 111.3 %copy-start.1 = (bf16[1024,1536]{1,0:T(8,128)(2,1)S(1)}, bf16[1024,1536]{1,0:T(8,128)(2,1)}, u32[]{:S(2)}) copy-start(bf16[1024,1536]{1,0:T(8,128)(2,1)} %param.18) | copy-start | bytes 9437188
  (30 other events, 374.2 us)
Sparse Core Ops, SparseCore 0:
  9.6 88.8 all-gather.7
  113.8 57.9 all-gather.5
  418.9 77.5 all-reduce.2
  498.6 138.0 reduce-scatter.1
